TPU v7x, 256 devices: a whole 4x4x8 slice. The times are simulated.
256 devices in a mesh: node: 4 (over y), rank: 32 (over z, x), chip: 2 (over core).
Axes of the slice: x: 4, y: 4, z: 8, core: 2. Of those that a mesh axis runs over, the one named last changes fastest.
Arguments:
- velocity: float32 [3, 8388608], P(None, ('node', 'rank', 'chip')), may hold values from -6 to 6
- refine: int32 [256], P(('node', 'rank', 'chip')), may hold values from 0 to 6
Outputs:
- filtered: float32 [3, 8388608], P(None, ('node', 'rank', 'chip'))
All inputs are finite; a program needn't handle non-finite values.
Results may differ from a plain program's by a relative error of at most 0.00002.
Values sent between devices are 32-bit elements; how exact they have to be, the bound alone decides.
A program may use at most 128 MiB of HBM per device.

v0:
```python
import jax
import jax.numpy as jnp
import numpy as np
from jax import lax
from jax.sharding import PartitionSpec as P

BLOCK = 32768
LEVELS = 6


def passed_along(x, axis, by):
    devices = lax.axis_size(axis)
    return lax.ppermute(x, axis, [(i, (i + by) % devices) for i in range(devices)])


def predict(before, here, after, later):
    return (-before + 9.0 * here + 9.0 * after - later) / 16.0


def to_phases(field):
    phases = 2**LEVELS
    return field.reshape(field.shape[0], -1, phases).transpose(0, 2, 1)


def from_phases(field):
    return field.transpose(0, 2, 1).reshape(field.shape[0], -1)


def first_values(field, count):
    phases = field.shape[1]
    index = np.arange(count)
    return field[:, index % phases, index // phases]


def last_values(field, count):
    phases = field.shape[1]
    total = phases * field.shape[2]
    index = np.arange(total - count, total)
    return field[:, index % phases, index // phases]


def shift_up(field, edge):
    moved = jnp.concatenate([field[:, 0, 1:], edge[:, None]], axis=1)
    return jnp.concatenate([field[:, 1:, :], moved[:, None, :]], axis=1)


def shift_down(field, edge):
    moved = jnp.concatenate([edge[:, None], field[:, -1, :-1]], axis=1)
    return jnp.concatenate([moved[:, None, :], field[:, :-1, :]], axis=1)


def lane_keep(levels_held, level_index):
    return jnp.repeat(levels_held, BLOCK // 2**LEVELS) > level_index


def forward_level(current, left_rim, right_rim):
    even_part = current[:, 0::2, :]
    odd_part = current[:, 1::2, :]
    head = first_values(even_part, 2)
    detail_before = left_rim[:, 3] - predict(left_rim[:, 0], left_rim[:, 2], head[:, 0], head[:, 1])
    even_next = shift_up(even_part, right_rim[:, 0])
    detail = odd_part - predict(
        shift_down(even_part, left_rim[:, 2]),
        even_part,
        even_next,
        shift_up(even_next, right_rim[:, 2]),
    )
    scaling = even_part + (shift_down(detail, detail_before) + detail) / 4.0
    return (scaling, detail)


def inverse_level(scaling, detail, left_rim, right_rim):
    detail_last = last_values(detail, 1)[:, 0]
    even_before = left_rim[0][:, 1] - (left_rim[1][:, 0] + left_rim[1][:, 1]) / 4.0
    even_after = right_rim[0][:, 0] - (detail_last + right_rim[1][:, 0]) / 4.0
    even_later = right_rim[0][:, 1] - (right_rim[1][:, 0] + right_rim[1][:, 1]) / 4.0
    even_part = scaling - (shift_down(detail, left_rim[1][:, 1]) + detail) / 4.0
    even_next = shift_up(even_part, even_after)
    odd_part = detail + predict(
        shift_down(even_part, even_before), even_part, even_next, shift_up(even_next, even_later)
    )
    stacked = jnp.stack([even_part, odd_part], axis=2)
    return stacked.reshape(scaling.shape[0], 2 * scaling.shape[1], scaling.shape[2])


def inverse_rims(scaling, detail):
    return (
        jnp.stack([last_values(scaling, 2), last_values(detail, 2)]),
        jnp.stack([first_values(scaling, 2), first_values(detail, 2)]),
    )


def per_device(velocity, refine):
    current = to_phases(velocity)
    details = []
    for level_index in range(LEVELS):
        left_rim = passed_along(last_values(current, 4), ("node", "rank", "chip"), 1)
        right_rim = passed_along(first_values(current, 4), ("node", "rank", "chip"), -1)
        scaling, detail = forward_level(current, left_rim, right_rim)
        details.append(jnp.where(lane_keep(refine, level_index)[None, None, :], detail, 0.0))
        current = scaling
    for level_index in reversed(range(LEVELS)):
        low_rim, high_rim = inverse_rims(current, details[level_index])
        left_rim = passed_along(low_rim, ("node", "rank", "chip"), 1)
        right_rim = passed_along(high_rim, ("node", "rank", "chip"), -1)
        current = inverse_level(current, details[level_index], left_rim, right_rim)
    return from_phases(current)


def solution(mesh):
    return jax.shard_map(
        per_device,
        mesh=mesh,
        in_specs=(P(None, ("node", "rank", "chip")), P(("node", "rank", "chip"))),
        out_specs=P(None, ("node", "rank", "chip")),
        check_vma=False,
    )
```

profile of v0, /device:TPU:0, one launch (start us, length us, event | category | flops | bytes accessed | tf_op | source)
XLA Modules:
  0.0 220.6 jit_solution(481179980602574905)
XLA Ops:
  0.0 1.5 reshape.156
  1.5 8.3 %copy.1208 = f32[3,64,512]{0,2,1:T(8,128)} copy(f32[3,64,512]{1,2,0:T(8,128)S(1)} %bitcast.424) | data formatting | bytes 786432 | tf_op jit(solution)/shard_map/transpose | solution.py:22
  9.8 1.4 gather_fusion
  11.3 1.3 gather_fusion.2
  12.5 8.2 %collective-permute-start.1 = (f32[3,4]{0,1:T(4,128)S(1)}, f32[3,4]{0,1:T(4,128)S(1)}, u32[]{:S(2)}, u32[]{:S(2)}) collective-permute-start(f32[3,4]{0,1:T(4,128)S(1)} %bitcast.505), channel_id=1, source_target_pairs={{0,255},{1,0},{2,1},{3,2},{4,3},{5,4},{6,5},{7,6},{8,7},{9,8},{10,... | collective-permute-start | bytes 152 | tf_op jit(solution)/shard_map/ppermute | solution.py:13
  21.2 4.7 %copy.1210 = f32[3,32,512]{0,2,1:T(8,128)} copy(f32[3,32,512]{2,1,0:T(8,128)S(1)} %slice.680) | data formatting | bytes 393216 | tf_op jit(solution)/shard_map/slice | solution.py:57
  26.3 1.3 gather_fusion.1
  29.3 4.7 %copy.1219 = f32[3,32,512]{0,2,1:T(8,128)} copy(f32[3,32,512]{2,1,0:T(8,128)S(1)} %fusion.15) | data formatting | bytes 393216 | tf_op jit(solution)/shard_map/add | solution.py:68
  34.0 2.7 %copy.1221 = f32[3,16,512]{0,2,1:T(8,128)} copy(f32[3,16,512]{2,1,0:T(8,128)S(1)} %slice.697) | data formatting | bytes 196608 | tf_op jit(solution)/shard_map/slice | solution.py:57
  36.9 4.7 %copy.1356 = f32[3,32,512]{0,2,1:T(8,128)} copy(f32[3,32,512]{2,1,0:T(8,128)S(1)} %get-tuple-element.81) | data formatting | bytes 393216 | tf_op jit(solution)/shard_map/jit(_where)/select_n | solution.py:100
  42.2 1.2 gather_fusion.4
  43.6 1.3 gather_fusion.5
  44.9 1.3 gather_fusion.3
  46.3 7.2 %collective-permute-start.3 = (f32[3,4]{0,1:T(4,128)S(1)}, f32[3,4]{0,1:T(4,128)S(1)}, u32[]{:S(2)}, u32[]{:S(2)}) collective-permute-start(f32[3,4]{0,1:T(4,128)S(1)} %bitcast.508), channel_id=1, source_target_pairs={{0,255},{1,0},{2,1},{3,2},{4,3},{5,4},{6,5},{7,6},{8,7},{9,8},{10,... | collective-permute-start | bytes 152 | tf_op jit(solution)/shard_map/ppermute | solution.py:13
  53.5 1.8 gather_fusion.41
  55.3 2.0 gather_fusion.39
  58.0 2.7 %copy.1230 = f32[3,16,512]{0,2,1:T(8,128)} copy(f32[3,16,512]{2,1,0:T(8,128)S(1)} %fusion.34) | data formatting | bytes 196608 | tf_op jit(solution)/shard_map/add | solution.py:68
  61.6 2.7 %copy.1339 = f32[3,16,512]{0,2,1:T(8,128)} copy(f32[3,16,512]{2,1,0:T(8,128)S(1)} %get-tuple-element.79) | data formatting | bytes 196608 | tf_op jit(solution)/shard_map/jit(_where)/select_n | solution.py:100
  64.9 1.3 gather_fusion.8
  66.1 1.3 gather_fusion.6
  68.2 7.2 %collective-permute-start.5 = (f32[3,4]{0,1:T(4,128)S(1)}, f32[3,4]{0,1:T(4,128)S(1)}, u32[]{:S(2)}, u32[]{:S(2)}) collective-permute-start(f32[3,4]{0,1:T(4,128)S(1)} %bitcast.506), channel_id=1, source_target_pairs={{0,255},{1,0},{2,1},{3,2},{4,3},{5,4},{6,5},{7,6},{8,7},{9,8},{10,... | collective-permute-start | bytes 152 | tf_op jit(solution)/shard_map/ppermute | solution.py:13
  75.4 1.8 gather_fusion.37
  77.2 1.9 gather_fusion.35
  80.5 1.9 copy.1241
  82.9 0.7 fusion.137
  86.7 1.8 gather_fusion.11
  88.5 2.0 gather_fusion.9
  90.5 1.3 copy.1242
  91.8 1.2 gather_fusion.10
  93.0 0.8 copy.1244
  93.7 0.7 copy.1516
  94.4 7.2 %collective-permute-start.7 = (f32[3,4]{0,1:T(4,128)}, f32[3,4]{0,1:T(4,128)S(1)}, u32[]{:S(2)}, u32[]{:S(2)}) collective-permute-start(f32[3,4]{0,1:T(4,128)} %bitcast.507), channel_id=1, source_target_pairs={{0,255},{1,0},{2,1},{3,2},{4,3},{5,4},{6,5},{7,6},{8,7},{9,8},{10,... | collective-permute-start | bytes 152 | tf_op jit(solution)/shard_map/ppermute | solution.py:13
  101.6 0.7 copy.1532
  102.3 0.7 copy.1531
  103.6 0.7 gather_fusion.31
  104.3 0.7 copy.1512
  104.9 0.9 multiply_subtract_fusion.13
  106.3 0.8 broadcast_select_fusion.3
  109.1 0.7 gather_fusion.12
  110.6 7.2 %collective-permute-start.9 = (f32[3,4]{1,0:T(4,128)S(1)}, f32[3,4]{1,0:T(4,128)S(1)}, u32[]{:S(2)}, u32[]{:S(2)}) collective-permute-start(f32[3,4]{1,0:T(4,128)S(1)} %bitcast.516), channel_id=1, source_target_pairs={{0,255},{1,0},{2,1},{3,2},{4,3},{5,4},{6,5},{7,6},{8,7},{9,8},{10,... | collective-permute-start | bytes 152 | tf_op jit(solution)/shard_map/ppermute | solution.py:13
  118.4 0.7 gather_fusion.27
  121.0 7.1 %collective-permute-start.11 = (f32[3,4]{1,0:T(4,128)S(1)}, f32[3,4]{1,0:T(4,128)S(1)}, u32[]{:S(2)}, u32[]{:S(2)}) collective-permute-start(f32[3,4]{1,0:T(4,128)S(1)} %bitcast.515), channel_id=1, source_target_pairs={{0,255},{1,0},{2,1},{3,2},{4,3},{5,4},{6,5},{7,6},{8,7},{9,8},{10,... | collective-permute-start | bytes 152 | tf_op jit(solution)/shard_map/ppermute | solution.py:13
  129.5 0.7 gather_fusion.23
  130.4 6.9 %collective-permute-done.10 = f32[3,4]{1,0:T(4,128)S(1)} collective-permute-done((f32[3,4]{1,0:T(4,128)S(1)}, f32[3,4]{1,0:T(4,128)S(1)}, u32[]{:S(2)}, u32[]{:S(2)}) %collective-permute-start.10) | collective-permute-done | bytes 80 | tf_op jit(solution)/shard_map/ppermute | solution.py:13
  142.0 1.0 collective-permute-done.13
  143.4 6.7 %collective-permute-done.12 = f32[2,3,2]{1,2,0:T(2,128)S(1)} collective-permute-done((f32[2,3,2]{1,2,0:T(2,128)S(1)}, f32[2,3,2]{1,2,0:T(2,128)S(1)}, u32[]{:S(2)}, u32[]{:S(2)}) %collective-permute-start.12) | collective-permute-done | bytes 80 | tf_op jit(solution)/shard_map/ppermute | solution.py:13
  151.1 0.7 gather_fusion.22
  152.5 7.2 %collective-permute-start.15 = (f32[2,3,2]{1,2,0:T(2,128)S(1)}, f32[2,3,2]{1,2,0:T(2,128)S(1)}, u32[]{:S(2)}, u32[]{:S(2)}) collective-permute-start(f32[2,3,2]{1,2,0:T(2,128)S(1)} %pad_maximum_fusion.33), channel_id=1, source_target_pairs={{0,255},{1,0},{2,1},{3,2},{4,3},{5,4},{6,5},{7,6},{8,7},{9,8},{10,... | collective-permute-start | bytes 152 | tf_op jit(solution)/shard_map/ppermute | solution.py:13
  159.7 1.3 collective-permute-done.14
  163.9 7.2 %collective-permute-start.17 = (f32[2,3,2]{1,2,0:T(2,128)S(1)}, f32[2,3,2]{1,2,0:T(2,128)S(1)}, u32[]{:S(2)}, u32[]{:S(2)}) collective-permute-start(f32[2,3,2]{1,2,0:T(2,128)S(1)} %pad_maximum_fusion.35), channel_id=1, source_target_pairs={{0,255},{1,0},{2,1},{3,2},{4,3},{5,4},{6,5},{7,6},{8,7},{9,8},{10,... | collective-permute-start | bytes 152 | tf_op jit(solution)/shard_map/ppermute | solution.py:13
  171.0 1.3 collective-permute-done.16
  175.7 7.2 %collective-permute-start.19 = (f32[2,3,2]{1,2,0:T(2,128)S(1)}, f32[2,3,2]{1,2,0:T(2,128)S(1)}, u32[]{:S(2)}, u32[]{:S(2)}) collective-permute-start(f32[2,3,2]{1,2,0:T(2,128)S(1)} %pad_maximum_fusion.37), channel_id=1, source_target_pairs={{0,255},{1,0},{2,1},{3,2},{4,3},{5,4},{6,5},{7,6},{8,7},{9,8},{10,... | collective-permute-start | bytes 152 | tf_op jit(solution)/shard_map/ppermute | solution.py:13
  182.8 1.3 collective-permute-done.18
  185.5 2.7 %copy.1338 = f32[3,16,512]{0,2,1:T(8,128)} copy(f32[3,16,512]{2,1,0:T(8,128)S(1)} %reshape.160) | data formatting | bytes 196608 | tf_op jit(solution)/shard_map/reshape | solution.py:83
  188.3 1.5 gather_fusion.34
  189.7 1.3 gather_fusion.36
  191.1 7.1 %collective-permute-start.21 = (f32[2,3,2]{1,2,0:T(2,128)S(1)}, f32[2,3,2]{1,2,0:T(2,128)S(1)}, u32[]{:S(2)}, u32[]{:S(2)}) collective-permute-start(f32[2,3,2]{1,2,0:T(2,128)S(1)} %pad_maximum_fusion.39), channel_id=1, source_target_pairs={{0,255},{1,0},{2,1},{3,2},{4,3},{5,4},{6,5},{7,6},{8,7},{9,8},{10,... | collective-permute-start | bytes 152 | tf_op jit(solution)/shard_map/ppermute | solution.py:13
  198.2 1.3 collective-permute-done.20
  201.2 4.7 %copy.1355 = f32[3,32,512]{0,2,1:T(8,128)} copy(f32[3,32,512]{2,1,0:T(8,128)S(1)} %reshape.161) | data formatting | bytes 393216 | tf_op jit(solution)/shard_map/reshape | solution.py:83
  205.9 1.4 gather_fusion.38
  207.3 1.3 gather_fusion.40
  208.7 7.1 %collective-permute-start.23 = (f32[2,3,2]{1,2,0:T(2,128)S(1)}, f32[2,3,2]{1,2,0:T(2,128)S(1)}, u32[]{:S(2)}, u32[]{:S(2)}) collective-permute-start(f32[2,3,2]{1,2,0:T(2,128)S(1)} %pad_maximum_fusion.41), channel_id=1, source_target_pairs={{0,255},{1,0},{2,1},{3,2},{4,3},{5,4},{6,5},{7,6},{8,7},{9,8},{10,... | collective-permute-start | bytes 152 | tf_op jit(solution)/shard_map/ppermute | solution.py:13
  215.9 1.3 collective-permute-done.22
  219.5 1.2 reshape.163
  (444 shorter events, 36.3 us)
Async XLA Ops:
  1.5 8.3 %copy-start.14 = (s32[4]{0:T(128)S(1)}, s32[4]{0:T(128)}, u32[]{:S(2)}) copy-start(s32[4]{0:T(128)} %constant.935) | copy-start | bytes 52
  11.2 17.1 %collective-permute-start = (f32[3,4]{1,0:T(4,128)S(1)}, f32[3,4]{1,0:T(4,128)S(1)}, u32[]{:S(2)}, u32[]{:S(2)}) collective-permute-start(f32[3,4]{1,0:T(4,128)S(1)} %bitcast.509), channel_id=1, source_target_pairs={{0,1},{1,2},{2,3},{3,4},{4,5},{5,6},{6,7},{7,8},{8,9},{9,10},{10,1... | collective-permute-start | bytes 152 | tf_op jit(solution)/shard_map/ppermute | solution.py:13
  12.5 16.0 %collective-permute-start.1 = (f32[3,4]{0,1:T(4,128)S(1)}, f32[3,4]{0,1:T(4,128)S(1)}, u32[]{:S(2)}, u32[]{:S(2)}) collective-permute-start(f32[3,4]{0,1:T(4,128)S(1)} %bitcast.505), channel_id=1, source_target_pairs={{0,255},{1,0},{2,1},{3,2},{4,3},{5,4},{6,5},{7,6},{8,7},{9,8},{10,... | collective-permute-start | bytes 152 | tf_op jit(solution)/shard_map/ppermute | solution.py:13
  36.8 8.0 %copy-start.13 = (s32[4]{0:T(128)S(1)}, s32[4]{0:T(128)}, u32[]{:S(2)}) copy-start(s32[4]{0:T(128)} %constant.959) | copy-start | bytes 52
  36.9 18.4 %copy-start.6 = (s32[2]{0:T(128)S(1)}, s32[2]{0:T(128)}, u32[]{:S(2)}) copy-start(s32[2]{0:T(128)} %constant.1239) | copy-start | bytes 28
  46.3 11.0 %collective-permute-start.2 = (f32[3,4]{1,0:T(4,128)S(1)}, f32[3,4]{1,0:T(4,128)S(1)}, u32[]{:S(2)}, u32[]{:S(2)}) collective-permute-start(f32[3,4]{1,0:T(4,128)S(1)} %bitcast.514), channel_id=1, source_target_pairs={{0,1},{1,2},{2,3},{3,4},{4,5},{5,6},{6,7},{7,8},{8,9},{9,10},{10,1... | collective-permute-start | bytes 152 | tf_op jit(solution)/shard_map/ppermute | solution.py:13
  46.3 11.1 %collective-permute-start.3 = (f32[3,4]{0,1:T(4,128)S(1)}, f32[3,4]{0,1:T(4,128)S(1)}, u32[]{:S(2)}, u32[]{:S(2)}) collective-permute-start(f32[3,4]{0,1:T(4,128)S(1)} %bitcast.508), channel_id=1, source_target_pairs={{0,255},{1,0},{2,1},{3,2},{4,3},{5,4},{6,5},{7,6},{8,7},{9,8},{10,... | collective-permute-start | bytes 152 | tf_op jit(solution)/shard_map/ppermute | solution.py:13
  60.7 5.4 %copy-start.12 = (s32[4]{0:T(128)S(1)}, s32[4]{0:T(128)}, u32[]{:S(2)}) copy-start(s32[4]{0:T(128)} %constant.983) | copy-start | bytes 52
  60.7 16.5 %copy-start.8 = (s32[2]{0:T(128)S(1)}, s32[2]{0:T(128)}, u32[]{:S(2)}) copy-start(s32[2]{0:T(128)} %constant.1207) | copy-start | bytes 28
  67.6 12.2 %collective-permute-start.4 = (f32[3,4]{1,0:T(4,128)S(1)}, f32[3,4]{1,0:T(4,128)S(1)}, u32[]{:S(2)}, u32[]{:S(2)}) collective-permute-start(f32[3,4]{1,0:T(4,128)S(1)} %bitcast.511), channel_id=1, source_target_pairs={{0,1},{1,2},{2,3},{3,4},{4,5},{5,6},{6,7},{7,8},{8,9},{9,10},{10,1... | collective-permute-start | bytes 152 | tf_op jit(solution)/shard_map/ppermute | solution.py:13
  68.2 11.7 %collective-permute-start.5 = (f32[3,4]{0,1:T(4,128)S(1)}, f32[3,4]{0,1:T(4,128)S(1)}, u32[]{:S(2)}, u32[]{:S(2)}) collective-permute-start(f32[3,4]{0,1:T(4,128)S(1)} %bitcast.506), channel_id=1, source_target_pairs={{0,255},{1,0},{2,1},{3,2},{4,3},{5,4},{6,5},{7,6},{8,7},{9,8},{10,... | collective-permute-start | bytes 152 | tf_op jit(solution)/shard_map/ppermute | solution.py:13
  84.2 22.1 %copy-start = (f32[3,3,512]{2,1,0:T(4,128)}, f32[3,3,512]{2,1,0:T(4,128)S(1)}, u32[]{:S(2)}) copy-start(f32[3,3,512]{2,1,0:T(4,128)S(1)} %get-tuple-element.122) | copy-start | bytes 55300
  91.8 13.1 %collective-permute-start.6 = (f32[3,4]{1,0:T(4,128)}, f32[3,4]{1,0:T(4,128)}, u32[]{:S(2)}, u32[]{:S(2)}) collective-permute-start(f32[3,4]{1,0:T(4,128)} %bitcast.512), channel_id=1, source_target_pairs={{0,1},{1,2},{2,3},{3,4},{4,5},{5,6},{6,7},{7,8},{8,9},{9,10},{10,1... | collective-permute-start | bytes 152 | tf_op jit(solution)/shard_map/ppermute | solution.py:13
  94.4 11.5 %collective-permute-start.7 = (f32[3,4]{0,1:T(4,128)}, f32[3,4]{0,1:T(4,128)S(1)}, u32[]{:S(2)}, u32[]{:S(2)}) collective-permute-start(f32[3,4]{0,1:T(4,128)} %bitcast.507), channel_id=1, source_target_pairs={{0,255},{1,0},{2,1},{3,2},{4,3},{5,4},{6,5},{7,6},{8,7},{9,8},{10,... | collective-permute-start | bytes 152 | tf_op jit(solution)/shard_map/ppermute | solution.py:13
  107.3 55.4 %copy-start.11 = (s32[2]{0:T(128)S(1)}, s32[2]{0:T(128)}, u32[]{:S(2)}) copy-start(s32[2]{0:T(128)} %constant.1143) | copy-start | bytes 28
  109.9 9.5 %collective-permute-start.8 = (f32[3,4]{1,0:T(4,128)S(1)}, f32[3,4]{1,0:T(4,128)S(1)}, u32[]{:S(2)}, u32[]{:S(2)}) collective-permute-start(f32[3,4]{1,0:T(4,128)S(1)} %bitcast.510), channel_id=1, source_target_pairs={{0,1},{1,2},{2,3},{3,4},{4,5},{5,6},{6,7},{7,8},{8,9},{9,10},{10,1... | collective-permute-start | bytes 152 | tf_op jit(solution)/shard_map/ppermute | solution.py:13
  110.6 8.5 %collective-permute-start.9 = (f32[3,4]{1,0:T(4,128)S(1)}, f32[3,4]{1,0:T(4,128)S(1)}, u32[]{:S(2)}, u32[]{:S(2)}) collective-permute-start(f32[3,4]{1,0:T(4,128)S(1)} %bitcast.516), channel_id=1, source_target_pairs={{0,255},{1,0},{2,1},{3,2},{4,3},{5,4},{6,5},{7,6},{8,7},{9,8},{10,... | collective-permute-start | bytes 152 | tf_op jit(solution)/shard_map/ppermute | solution.py:13
  119.6 54.8 %copy-start.10 = (s32[2]{0:T(128)S(1)}, s32[2]{0:T(128)}, u32[]{:S(2)}) copy-start(s32[2]{0:T(128)} %constant.1175) | copy-start | bytes 28
  119.9 64.9 %copy-start.17 = (f32[3,1,1]{2,1,0:T(1,128)S(1)}, f32[3,1,1]{2,1,0:T(1,128)}, u32[]{:S(2)}) copy-start(f32[3,1,1]{2,1,0:T(1,128)} %slice.1146) | copy-start | bytes 40
  121.0 9.2 %collective-permute-start.11 = (f32[3,4]{1,0:T(4,128)S(1)}, f32[3,4]{1,0:T(4,128)S(1)}, u32[]{:S(2)}, u32[]{:S(2)}) collective-permute-start(f32[3,4]{1,0:T(4,128)S(1)} %bitcast.515), channel_id=1, source_target_pairs={{0,255},{1,0},{2,1},{3,2},{4,3},{5,4},{6,5},{7,6},{8,7},{9,8},{10,... | collective-permute-start | bytes 152 | tf_op jit(solution)/shard_map/ppermute | solution.py:13
  128.9 8.4 %collective-permute-start.10 = (f32[3,4]{1,0:T(4,128)S(1)}, f32[3,4]{1,0:T(4,128)S(1)}, u32[]{:S(2)}, u32[]{:S(2)}) collective-permute-start(f32[3,4]{1,0:T(4,128)S(1)} %bitcast.513), channel_id=1, source_target_pairs={{0,1},{1,2},{2,3},{3,4},{4,5},{5,6},{6,7},{7,8},{8,9},{9,10},{10,1... | collective-permute-start | bytes 152 | tf_op jit(solution)/shard_map/ppermute | solution.py:13
  141.4 1.6 collective-permute-start.13
  141.7 8.4 %collective-permute-start.12 = (f32[2,3,2]{1,2,0:T(2,128)S(1)}, f32[2,3,2]{1,2,0:T(2,128)S(1)}, u32[]{:S(2)}, u32[]{:S(2)}) collective-permute-start(f32[2,3,2]{1,2,0:T(2,128)S(1)} %pad_maximum_fusion.30), channel_id=1, source_target_pairs={{0,1},{1,2},{2,3},{3,4},{4,5},{5,6},{6,7},{7,8},{8,9},{9,10},{10,1... | collective-permute-start | bytes 152 | tf_op jit(solution)/shard_map/ppermute | solution.py:13
  152.4 8.5 %collective-permute-start.14 = (f32[2,3,2]{1,2,0:T(2,128)S(1)}, f32[2,3,2]{1,2,0:T(2,128)S(1)}, u32[]{:S(2)}, u32[]{:S(2)}) collective-permute-start(f32[2,3,2]{1,2,0:T(2,128)S(1)} %pad_maximum_fusion.32), channel_id=1, source_target_pairs={{0,1},{1,2},{2,3},{3,4},{4,5},{5,6},{6,7},{7,8},{8,9},{9,10},{10,1... | collective-permute-start | bytes 152 | tf_op jit(solution)/shard_map/ppermute | solution.py:13
  152.5 8.7 %collective-permute-start.15 = (f32[2,3,2]{1,2,0:T(2,128)S(1)}, f32[2,3,2]{1,2,0:T(2,128)S(1)}, u32[]{:S(2)}, u32[]{:S(2)}) collective-permute-start(f32[2,3,2]{1,2,0:T(2,128)S(1)} %pad_maximum_fusion.33), channel_id=1, source_target_pairs={{0,255},{1,0},{2,1},{3,2},{4,3},{5,4},{6,5},{7,6},{8,7},{9,8},{10,... | collective-permute-start | bytes 152 | tf_op jit(solution)/shard_map/ppermute | solution.py:13
  163.8 8.5 %collective-permute-start.16 = (f32[2,3,2]{1,2,0:T(2,128)S(1)}, f32[2,3,2]{1,2,0:T(2,128)S(1)}, u32[]{:S(2)}, u32[]{:S(2)}) collective-permute-start(f32[2,3,2]{1,2,0:T(2,128)S(1)} %pad_maximum_fusion.34), channel_id=1, source_target_pairs={{0,1},{1,2},{2,3},{3,4},{4,5},{5,6},{6,7},{7,8},{8,9},{9,10},{10,1... | collective-permute-start | bytes 152 | tf_op jit(solution)/shard_map/ppermute | solution.py:13
  163.9 8.8 %collective-permute-start.17 = (f32[2,3,2]{1,2,0:T(2,128)S(1)}, f32[2,3,2]{1,2,0:T(2,128)S(1)}, u32[]{:S(2)}, u32[]{:S(2)}) collective-permute-start(f32[2,3,2]{1,2,0:T(2,128)S(1)} %pad_maximum_fusion.35), channel_id=1, source_target_pairs={{0,255},{1,0},{2,1},{3,2},{4,3},{5,4},{6,5},{7,6},{8,7},{9,8},{10,... | collective-permute-start | bytes 152 | tf_op jit(solution)/shard_map/ppermute | solution.py:13
  173.6 14.6 %copy-start.9 = (s32[2]{0:T(128)S(1)}, s32[2]{0:T(128)}, u32[]{:S(2)}) copy-start(s32[2]{0:T(128)} %constant.1207) | copy-start | bytes 28
  173.7 17.3 %copy-start.5 = (f32[2,3]{1,0:T(2,128)S(1)}, f32[2,3]{1,0:T(2,128)}, u32[]{:S(2)}) copy-start(f32[2,3]{1,0:T(2,128)} %gather_fusion.35) | copy-start | bytes 76
  173.7 17.4 %copy-start.4 = (f32[2,3]{1,0:T(2,128)S(1)}, f32[2,3]{1,0:T(2,128)}, u32[]{:S(2)}) copy-start(f32[2,3]{1,0:T(2,128)} %gather_fusion.37) | copy-start | bytes 76
  173.7 25.9 %copy-start.1 = (f32[3,1,511]{2,0,1:T(4,128)S(1)}, f32[3,1,511]{2,0,1:T(4,128)}, u32[]{:S(2)}) copy-start(f32[3,1,511]{2,0,1:T(4,128)} %copy.1510) | copy-start | bytes 18400
  173.7 26.5 %copy-start.16 = (f32[3,1,1]{2,1,0:T(1,128)S(1)}, f32[3,1,1]{2,1,0:T(1,128)}, u32[]{:S(2)}) copy-start(f32[3,1,1]{2,1,0:T(1,128)} %slice.1160) | copy-start | bytes 40
  175.6 8.5 %collective-permute-start.18 = (f32[2,3,2]{1,2,0:T(2,128)S(1)}, f32[2,3,2]{1,2,0:T(2,128)S(1)}, u32[]{:S(2)}, u32[]{:S(2)}) collective-permute-start(f32[2,3,2]{1,2,0:T(2,128)S(1)} %pad_maximum_fusion.36), channel_id=1, source_target_pairs={{0,1},{1,2},{2,3},{3,4},{4,5},{5,6},{6,7},{7,8},{8,9},{9,10},{10,1... | collective-permute-start | bytes 152 | tf_op jit(solution)/shard_map/ppermute | solution.py:13
  175.7 8.8 %collective-permute-start.19 = (f32[2,3,2]{1,2,0:T(2,128)S(1)}, f32[2,3,2]{1,2,0:T(2,128)S(1)}, u32[]{:S(2)}, u32[]{:S(2)}) collective-permute-start(f32[2,3,2]{1,2,0:T(2,128)S(1)} %pad_maximum_fusion.37), channel_id=1, source_target_pairs={{0,255},{1,0},{2,1},{3,2},{4,3},{5,4},{6,5},{7,6},{8,7},{9,8},{10,... | collective-permute-start | bytes 152 | tf_op jit(solution)/shard_map/ppermute | solution.py:13
  191.0 8.5 %collective-permute-start.20 = (f32[2,3,2]{1,2,0:T(2,128)S(1)}, f32[2,3,2]{1,2,0:T(2,128)S(1)}, u32[]{:S(2)}, u32[]{:S(2)}) collective-permute-start(f32[2,3,2]{1,2,0:T(2,128)S(1)} %pad_maximum_fusion.38), channel_id=1, source_target_pairs={{0,1},{1,2},{2,3},{3,4},{4,5},{5,6},{6,7},{7,8},{8,9},{9,10},{10,1... | collective-permute-start | bytes 152 | tf_op jit(solution)/shard_map/ppermute | solution.py:13
  191.1 8.8 %collective-permute-start.21 = (f32[2,3,2]{1,2,0:T(2,128)S(1)}, f32[2,3,2]{1,2,0:T(2,128)S(1)}, u32[]{:S(2)}, u32[]{:S(2)}) collective-permute-start(f32[2,3,2]{1,2,0:T(2,128)S(1)} %pad_maximum_fusion.39), channel_id=1, source_target_pairs={{0,255},{1,0},{2,1},{3,2},{4,3},{5,4},{6,5},{7,6},{8,7},{9,8},{10,... | collective-permute-start | bytes 152 | tf_op jit(solution)/shard_map/ppermute | solution.py:13
  201.2 4.8 %copy-start.7 = (s32[2]{0:T(128)S(1)}, s32[2]{0:T(128)}, u32[]{:S(2)}) copy-start(s32[2]{0:T(128)} %constant.1239) | copy-start | bytes 28
  201.2 7.4 %copy-start.3 = (f32[2,3]{1,0:T(2,128)S(1)}, f32[2,3]{1,0:T(2,128)}, u32[]{:S(2)}) copy-start(f32[2,3]{1,0:T(2,128)} %gather_fusion.39) | copy-start | bytes 76
  201.2 7.5 %copy-start.2 = (f32[2,3]{1,0:T(2,128)S(1)}, f32[2,3]{1,0:T(2,128)}, u32[]{:S(2)}) copy-start(f32[2,3]{1,0:T(2,128)} %gather_fusion.41) | copy-start | bytes 76
  201.2 16.7 %copy-start.15 = (f32[3,1,1]{2,1,0:T(1,128)S(1)}, f32[3,1,1]{2,1,0:T(1,128)}, u32[]{:S(2)}) copy-start(f32[3,1,1]{2,1,0:T(1,128)} %slice.1174) | copy-start | bytes 40
  208.6 8.5 %collective-permute-start.22 = (f32[2,3,2]{1,2,0:T(2,128)S(1)}, f32[2,3,2]{1,2,0:T(2,128)S(1)}, u32[]{:S(2)}, u32[]{:S(2)}) collective-permute-start(f32[2,3,2]{1,2,0:T(2,128)S(1)} %pad_maximum_fusion.40), channel_id=1, source_target_pairs={{0,1},{1,2},{2,3},{3,4},{4,5},{5,6},{6,7},{7,8},{8,9},{9,10},{10,1... | collective-permute-start | bytes 152 | tf_op jit(solution)/shard_map/ppermute | solution.py:13
  208.7 8.8 %collective-permute-start.23 = (f32[2,3,2]{1,2,0:T(2,128)S(1)}, f32[2,3,2]{1,2,0:T(2,128)S(1)}, u32[]{:S(2)}, u32[]{:S(2)}) collective-permute-start(f32[2,3,2]{1,2,0:T(2,128)S(1)} %pad_maximum_fusion.41), channel_id=1, source_target_pairs={{0,255},{1,0},{2,1},{3,2},{4,3},{5,4},{6,5},{7,6},{8,7},{9,8},{10,... | collective-permute-start | bytes 152 | tf_op jit(solution)/shard_map/ppermute | solution.py:13
where the time goes:
time: 221 us
  local copies, waits for them, and re-layouts  110 us (50%)
  starting transfers between devices  80.8 us (37%)
  waiting for transfers between devices  21.1 us (10%)
  other arithmetic  6.97 us (3%)
    ppermute x24, starting transfers between devices, passed_along(): lax.ppermute(x, axis, [(i, (i + by) % devices) for i in range(devices)])  80.8 us
    gather x32, local copies, waits for them, and re-layouts, first_values(): return field[:, index % phases, index // phases]  24.2 us
    gather x24, local copies, waits for them, and re-layouts, last_values(): return field[:, index % phases, index // phases]  21.3 us
    ppermute x24, waiting for transfers between devices, passed_along(): lax.ppermute(x, axis, [(i, (i + by) % devices) for i in range(devices)])  21.1 us
    add x6, local copies, waits for them, and re-layouts, forward_level(): scaling = even_part + (shift_down(detail, detail_before) + detail) / 4.0  10.1 us
    unnamed x115, local copies, waits for them, and re-layouts  9.49 us
    reshape x10, local copies, waits for them, and re-layouts, inverse_level(): stacked.reshape(scaling.shape[0], 2 * scaling.shape[1], scaling.shape[2])  9.18 us
    slice x11, local copies, waits for them, and re-layouts, forward_level(): even_part = current[:, 0::2, :]  9.1 us
  transfers between devices with their start and end apart: 24, of which 8 were waited for; matrix products, arithmetic and copies ran while one was open for 14% of the time, Pallas kernels for 0%

commit v1 on v0

v1 whole, which is shorter than its diff:
```python
import functools

import jax
import jax.numpy as jnp
from jax import lax
from jax.experimental import pallas as pl
from jax.experimental.pallas import tpu as pltpu
from jax.sharding import PartitionSpec as P

AXES = ("node", "rank", "chip")
LEVELS = 6
LANES = 128
COMP = 3
MESH = pl.DeviceIdType.MESH
HALO = 3
WIN = 16
CHUNK = 8


def coordinates(flat, sizes):
    nodes, ranks, chips = sizes
    return (flat // (ranks * chips), (flat // chips) % ranks, flat % chips)


def neighbours(sizes):
    nodes, ranks, chips = sizes
    total = nodes * ranks * chips
    me = (lax.axis_index("node") * ranks + lax.axis_index("rank")) * chips + lax.axis_index("chip")
    return (
        coordinates(lax.rem(me + total - 1, total), sizes),
        coordinates(lax.rem(me + 1, total), sizes),
    )


def after(row, carry_lane):
    rolled = pltpu.roll(row, LANES - 1, 1)
    carried = pltpu.roll(rolled, 7, 0)
    return jnp.where(carry_lane == LANES - 1, carried, rolled)


def before(row, carry_lane):
    rolled = pltpu.roll(row, 1, 1)
    carried = pltpu.roll(rolled, 1, 0)
    return jnp.where(carry_lane == 0, carried, rolled)


def predict(e):
    n = e.shape[0] - 3
    return (e[1 : n + 1] + e[2 : n + 2]) * (9.0 / 16.0) - (e[0:n] + e[3 : n + 3]) * (1.0 / 16.0)


def forward(values, details, level, lane):
    pairs = (LANES >> level) // 2
    src = values[level]
    e_first = src[pl.ds(0, 2, stride=2)]
    e_last = src[2 * pairs - 2]
    pre = before(e_last, lane)[None]
    post = jnp.stack([after(e_first[0], lane), after(e_first[1], lane)])
    step = min(CHUNK, pairs)
    d_prev = None
    e_zero, d_zero = None, None
    for at in range(0, pairs, step):
        lo, hi = max(at - 1, 0), min(at + step + 2, pairs)
        e = src[pl.ds(2 * lo, hi - lo, stride=2)]
        if at == 0:
            e = jnp.concatenate([pre, e], axis=0)
        need = step + 3 - e.shape[0]
        if need:
            e = jnp.concatenate([e, post[:need]], axis=0)
        o = src[pl.ds(2 * at + 1, step, stride=2)]
        d = o - predict(e)
        details[level][pl.ds(at, step)] = d
        here = e[1 : step + 1]
        if at == 0:
            e_zero, d_zero = here[0], d[0]
            if step > 1:
                values[level + 1][pl.ds(1, step - 1)] = here[1:] + (d[:-1] + d[1:]) * 0.25
        else:
            back = jnp.concatenate([d_prev, d[:-1]], axis=0)
            values[level + 1][pl.ds(at, step)] = here + (back + d) * 0.25
        d_prev = d[step - 1 :]
    values[level + 1][0] = e_zero + (before(d_prev[0], lane) + d_zero) * 0.25


def inverse(values, details, level, lane, keep):
    pairs = (LANES >> level) // 2
    dst = values[level]
    coarse = values[level + 1]

    def kept(at, count):
        d = details[level][pl.ds(at, count)]
        return jnp.where(keep[None], d, 0.0)

    step = min(CHUNK, pairs)
    k_before = before(kept(pairs - 1, 1)[0], lane)[None]
    back = k_before
    for at in range(0, pairs, step):
        k = kept(at, step)
        if step > 1:
            shifted = jnp.concatenate([back, k[:-1]], axis=0)
        else:
            shifted = back
        dst[pl.ds(2 * at, step, stride=2)] = coarse[pl.ds(at, step)] - (shifted + k) * 0.25
        back = k[step - 1 :]
    e_first = dst[pl.ds(0, 2, stride=2)]
    pre = before(dst[2 * pairs - 2], lane)[None]
    post = jnp.stack([after(e_first[0], lane), after(e_first[1], lane)])
    for at in range(0, pairs, step):
        lo, hi = max(at - 1, 0), min(at + step + 2, pairs)
        e = dst[pl.ds(2 * lo, hi - lo, stride=2)]
        if at == 0:
            e = jnp.concatenate([pre, e], axis=0)
        need = step + 3 - e.shape[0]
        if need:
            e = jnp.concatenate([e, post[:need]], axis=0)
        dst[pl.ds(2 * at + 1, step, stride=2)] = kept(at, step) + predict(e)


def kernel(
    sizes, x_ref, refine_ref, out_ref, xb, win, ob, wout, own_level, near_level, v0, v1, v2, v3, v4, v5, v6,
    d0, d1, d2, d3, d4, d5, in_sem, win_sem, level_sem, send_sem, recv_sem, out_sem,
):
    values = (v0, v1, v2, v3, v4, v5, v6)
    details = (d0, d1, d2, d3, d4, d5)
    rows = x_ref.shape[0]
    left, right = neighbours(sizes)
    barrier = pltpu.get_barrier_semaphore()
    for device in (left, right):
        pl.semaphore_signal(barrier, inc=1, device_id=device, device_id_type=MESH)

    loads = []
    for c in range(COMP):
        loads.append(pltpu.make_async_copy(x_ref.at[:, c, :], xb.at[c], in_sem.at[c]))
        loads.append(
            pltpu.make_async_copy(
                x_ref.at[pl.ds(0, 8), c, :], win.at[pl.ds(c * WIN + 8, 8), :], win_sem.at[c]
            )
        )
        loads.append(
            pltpu.make_async_copy(
                x_ref.at[pl.ds(rows - 8, 8), c, :],
                win.at[pl.ds((COMP + c) * WIN, 8), :],
                win_sem.at[COMP + c],
            )
        )
    loads.append(pltpu.make_async_copy(refine_ref, own_level, level_sem))
    for copy in loads:
        copy.start()

    pl.semaphore_wait(barrier, 2)
    sends = []
    for c in range(COMP):
        sends.append(
            pltpu.make_async_remote_copy(
                src_ref=x_ref.at[pl.ds(rows - 8, 8), c, :],
                dst_ref=win.at[pl.ds(c * WIN, 8), :],
                send_sem=send_sem.at[c],
                recv_sem=recv_sem.at[c],
                device_id=right,
                device_id_type=MESH,
            )
        )
        sends.append(
            pltpu.make_async_remote_copy(
                src_ref=x_ref.at[pl.ds(0, 8), c, :],
                dst_ref=win.at[pl.ds((COMP + c) * WIN + 8, 8), :],
                send_sem=send_sem.at[COMP + c],
                recv_sem=recv_sem.at[COMP + c],
                device_id=left,
                device_id_type=MESH,
            )
        )
    for side, device in ((0, right), (1, left)):
        sends.append(
            pltpu.make_async_remote_copy(
                src_ref=refine_ref,
                dst_ref=near_level.at[side],
                send_sem=send_sem.at[2 * COMP + side],
                recv_sem=recv_sem.at[2 * COMP + side],
                device_id=device,
                device_id_type=MESH,
            )
        )
    for copy in sends:
        copy.start()
    for copy in loads:
        copy.wait()

    for c in range(COMP):
        for half in range(2):
            block = xb[c, pl.ds(half * LANES, LANES), :]
            v0[:, 2 * c + half, :] = block.T
    for copy in sends:
        copy.wait()
    v0[:, 6, :] = win[...].T

    lane = lax.broadcasted_iota(jnp.int32, (8, LANES), 1)
    sublane = lax.broadcasted_iota(jnp.int32, (8, LANES), 0)
    own = own_level[0]
    from_left = (sublane == 6) & (lane < COMP * WIN) & (lane % WIN < 8)
    from_right = (sublane == 6) & (lane >= COMP * WIN) & (lane % WIN >= 8)
    level_of = jnp.where(from_left, near_level[0, 0], jnp.where(from_right, near_level[1, 0], own))

    for level in range(LEVELS):
        forward(values, details, level, lane)
    for level in reversed(range(LEVELS)):
        inverse(values, details, level, lane, level_of > level)

    stores = []
    for c in range(COMP):
        for half in range(2):
            ob[c, pl.ds(half * LANES, LANES), :] = v0[:, 2 * c + half, :].T
        stores.append(
            pltpu.make_async_copy(
                ob.at[c, pl.ds(HALO, rows - 2 * HALO), :], out_ref.at[pl.ds(HALO, rows - 2 * HALO), c, :], out_sem.at[c]
            )
        )
        stores[-1].start()
    wout[...] = v0[:, 6, :].T
    for c in range(COMP):
        stores.append(
            pltpu.make_async_copy(
                wout.at[pl.ds(c * WIN + 8, HALO), :], out_ref.at[pl.ds(0, HALO), c, :], out_sem.at[COMP + c]
            )
        )
        stores[-1].start()
        stores.append(
            pltpu.make_async_copy(
                wout.at[pl.ds((COMP + c) * WIN + 8 - HALO, HALO), :],
                out_ref.at[pl.ds(rows - HALO, HALO), c, :],
                out_sem.at[2 * COMP + c],
            )
        )
        stores[-1].start()
    for copy in stores:
        copy.wait()


def per_device(sizes, velocity, refine):
    rows = velocity.shape[1] // LANES
    x = velocity.reshape(COMP, rows, LANES).transpose(1, 0, 2)
    f32 = jnp.float32
    out = pl.pallas_call(
        functools.partial(kernel, sizes),
        out_shape=jax.ShapeDtypeStruct(x.shape, f32),
        in_specs=[pl.BlockSpec(memory_space=pl.ANY)] * 2,
        out_specs=pl.BlockSpec(memory_space=pl.ANY),
        scratch_shapes=[
            pltpu.VMEM((COMP, rows, LANES), f32),
            pltpu.VMEM((LANES, LANES), f32),
            pltpu.VMEM((COMP, rows, LANES), f32),
            pltpu.VMEM((LANES, LANES), f32),
            pltpu.SMEM((1,), jnp.int32),
            pltpu.SMEM((2, 1), jnp.int32),
        ]
        + [pltpu.VMEM((LANES >> level, 8, LANES), f32) for level in range(LEVELS + 1)]
        + [pltpu.VMEM(((LANES >> level) // 2, 8, LANES), f32) for level in range(LEVELS)]
        + [
            pltpu.SemaphoreType.DMA((COMP,)),
            pltpu.SemaphoreType.DMA((2 * COMP,)),
            pltpu.SemaphoreType.DMA,
            pltpu.SemaphoreType.DMA((2 * COMP + 2,)),
            pltpu.SemaphoreType.DMA((2 * COMP + 2,)),
            pltpu.SemaphoreType.DMA((3 * COMP,)),
        ],
        compiler_params=pltpu.CompilerParams(collective_id=0, has_side_effects=True),
    )(x, refine)
    return out.transpose(1, 0, 2).reshape(velocity.shape)


def solution(mesh):
    sizes = tuple(mesh.shape[name] for name in AXES)
    return jax.shard_map(
        functools.partial(per_device, sizes),
        mesh=mesh,
        in_specs=(P(None, AXES), P(AXES)),
        out_specs=P(None, AXES),
        check_vma=False,
    )
```

time: 221 us -> 17.9 us (0.08)
  the two profiles are of different devices: /device:TPU:0 before, /device:TPU:1 now
where the time goes in v1:
time: 17.9 us; the launch traced here: 17.8 us
  Pallas kernels  15.2 us (85%)
  local copies, waits for them, and re-layouts  1.93 us (11%)
  between operations  0.66 us (4%)
    pallas_call x1, Pallas kernels, per_device(): pl.pallas_call(functools.partial(kernel, sizes), out_shape=jax.ShapeDtype...  15.2 us
    unnamed x1, local copies, waits for them, and re-layouts  1.93 us

profile of v1, /device:TPU:1, one launch (start us, length us, event | category | flops | bytes accessed | tf_op | source)
XLA Modules:
  0.0 17.8 jit_solution(3786366976521423862)
XLA Ops:
  0.7 15.2 %shard_map.28 = f32[256,3,128]{2,1,0:T(4,128)} custom-call(f32[256,3,128]{2,1,0:T(4,128)} %bitcast.7, s32[1]{0:T(128)S(6)} %copy.4.refine_ref), custom_call_target="tpu_custom_call" | custom-call | tf_op jit(solution)/shard_map/pallas_call | solution.py:243
  15.9 1.9 %copy.5 = f32[3,32768]{1,0:T(4,128)} copy(f32[3,32768]{1,0:T(4,128)} %bitcast.6) | data formatting | bytes 786432

commit v2 on v1

v2 whole, which is shorter than its diff:
```python
import functools

import jax
import jax.numpy as jnp
from jax import lax
from jax.experimental import pallas as pl
from jax.experimental.pallas import tpu as pltpu
from jax.sharding import PartitionSpec as P

AXES = ("node", "rank", "chip")
LEVELS = 6
LANES = 128
COMP = 3
MESH = pl.DeviceIdType.MESH
HALO = 3
WIN = 16
CHUNK = 8
VMEM_LIMIT = 8 << 20


def coordinates(flat, sizes):
    nodes, ranks, chips = sizes
    return (flat // (ranks * chips), (flat // chips) % ranks, flat % chips)


def neighbours(sizes):
    nodes, ranks, chips = sizes
    total = nodes * ranks * chips
    me = (lax.axis_index("node") * ranks + lax.axis_index("rank")) * chips + lax.axis_index("chip")
    return (
        coordinates(lax.rem(me + total - 1, total), sizes),
        coordinates(lax.rem(me + 1, total), sizes),
    )


def after_with_carry(row, lane):
    rolled = pltpu.roll(row, LANES - 1, 1)
    carried = pltpu.roll(rolled, 7, 0)
    return jnp.where(lane == LANES - 1, carried, rolled)


def before_with_carry(row, lane):
    rolled = pltpu.roll(row, 1, 1)
    carried = pltpu.roll(rolled, 1, 0)
    return jnp.where(lane == 0, carried, rolled)


def after_in_window(row, lane):
    return pltpu.roll(row, LANES - 1, 1)


def before_in_window(row, lane):
    return pltpu.roll(row, 1, 1)


def predict(e):
    n = e.shape[0] - 3
    return (e[1 : n + 1] + e[2 : n + 2]) * (9.0 / 16.0) - (e[0:n] + e[3 : n + 3]) * (1.0 / 16.0)


def forward(values, details, level, lane, before, after):
    pairs = (LANES >> level) // 2
    src = values[level]
    e_first = src[pl.ds(0, 2, stride=2)]
    pre = before(src[2 * pairs - 2], lane)[None]
    post = jnp.stack([after(e_first[0], lane), after(e_first[1], lane)])
    step = min(CHUNK, pairs)
    d_prev, e_zero, d_zero = None, None, None
    for at in range(0, pairs, step):
        lo, hi = max(at - 1, 0), min(at + step + 2, pairs)
        e = src[pl.ds(2 * lo, hi - lo, stride=2)]
        if at == 0:
            e = jnp.concatenate([pre, e], axis=0)
        need = step + 3 - e.shape[0]
        if need:
            e = jnp.concatenate([e, post[:need]], axis=0)
        d = src[pl.ds(2 * at + 1, step, stride=2)] - predict(e)
        details[level][pl.ds(at, step)] = d
        here = e[1 : step + 1]
        if at == 0:
            e_zero, d_zero = here[0], d[0]
            values[level + 1][pl.ds(1, step - 1)] = here[1:] + (d[:-1] + d[1:]) * 0.25
        else:
            back = jnp.concatenate([d_prev, d[:-1]], axis=0)
            values[level + 1][pl.ds(at, step)] = here + (back + d) * 0.25
        d_prev = d[step - 1 :]
    values[level + 1][0] = e_zero + (before(d_prev[0], lane) + d_zero) * 0.25


def inverse(values, details, level, lane, keep, before, after):
    pairs = (LANES >> level) // 2
    dst = values[level]
    coarse = values[level + 1]

    def kept(at, count):
        return jnp.where(keep[None], details[level][pl.ds(at, count)], 0.0)

    step = min(CHUNK, pairs)
    back = before(kept(pairs - 1, 1)[0], lane)[None]
    for at in range(0, pairs, step):
        k = kept(at, step)
        shifted = jnp.concatenate([back, k[:-1]], axis=0)
        dst[pl.ds(2 * at, step, stride=2)] = coarse[pl.ds(at, step)] - (shifted + k) * 0.25
        back = k[step - 1 :]
    e_first = dst[pl.ds(0, 2, stride=2)]
    pre = before(dst[2 * pairs - 2], lane)[None]
    post = jnp.stack([after(e_first[0], lane), after(e_first[1], lane)])
    for at in range(0, pairs, step):
        lo, hi = max(at - 1, 0), min(at + step + 2, pairs)
        e = dst[pl.ds(2 * lo, hi - lo, stride=2)]
        if at == 0:
            e = jnp.concatenate([pre, e], axis=0)
        need = step + 3 - e.shape[0]
        if need:
            e = jnp.concatenate([e, post[:need]], axis=0)
        dst[pl.ds(2 * at + 1, step, stride=2)] = kept(at, step) + predict(e)


def transform(values, details, lane, level_of, before, after):
    for level in range(LEVELS):
        forward(values, details, level, lane, before, after)
    for level in reversed(range(LEVELS)):
        inverse(values, details, level, lane, level_of > level, before, after)


def lanes_and_sublanes():
    return (
        lax.broadcasted_iota(jnp.int32, (8, LANES), 1),
        lax.broadcasted_iota(jnp.int32, (8, LANES), 0),
    )


def exchange_kernel(sizes, x_ref, refine_ref, ob, win, level_ref, xb, own_level, near_level, *rest):
    values, details = rest[: LEVELS + 1], rest[LEVELS + 1 : 2 * LEVELS + 1]
    in_sem, win_sem, level_sem, send_sem, recv_sem = rest[2 * LEVELS + 1 :]
    rows = x_ref.shape[0]
    left, right = neighbours(sizes)
    barrier = pltpu.get_barrier_semaphore()
    pl.semaphore_signal(barrier, inc=1, device_id=left, device_id_type=MESH)

    loads = []
    for c in range(COMP):
        loads.append(pltpu.make_async_copy(x_ref.at[:, c, :], xb.at[c], in_sem.at[c]))
    ends = [pltpu.make_async_copy(refine_ref, own_level, level_sem)]
    for c in range(COMP):
        ends.append(
            pltpu.make_async_copy(
                x_ref.at[pl.ds(0, 8), c, :], win.at[pl.ds(c * WIN + 8, 8), :], win_sem.at[c]
            )
        )
        ends.append(
            pltpu.make_async_copy(
                x_ref.at[pl.ds(rows - 8, 8), c, :],
                win.at[pl.ds((COMP + c) * WIN, 8), :],
                win_sem.at[COMP + c],
            )
        )
    for copy in loads + ends:
        copy.start()

    def remote(src, dst, index, device):
        return pltpu.make_async_remote_copy(
            src_ref=src,
            dst_ref=dst,
            send_sem=send_sem.at[index],
            recv_sem=recv_sem.at[index],
            device_id=device,
            device_id_type=MESH,
        )

    to_right = [remote(refine_ref, near_level.at[0], 2 * COMP, right)]
    to_left = [remote(refine_ref, near_level.at[1], 2 * COMP + 1, left)]
    for c in range(COMP):
        to_right.append(
            remote(
                x_ref.at[pl.ds(rows - HALO, HALO), c, :],
                win.at[pl.ds(c * WIN + 8 - HALO, HALO), :],
                c,
                right,
            )
        )
        to_left.append(
            remote(
                x_ref.at[pl.ds(0, HALO), c, :],
                win.at[pl.ds((COMP + c) * WIN + 8, HALO), :],
                COMP + c,
                left,
            )
        )
    pl.semaphore_wait(barrier, 1)
    for copy in to_right:
        copy.start()
    for copy in loads + ends:
        copy.wait()

    lane, sublane = lanes_and_sublanes()
    own = own_level[0]
    for c in range(COMP):
        for half in range(2):
            values[0][:, 2 * c + half, :] = xb[c, pl.ds(half * LANES, LANES), :].T
    transform(
        values, details, lane, jnp.full((8, LANES), own, jnp.int32), before_with_carry, after_with_carry
    )
    for c in range(COMP):
        for half in range(2):
            ob[c, pl.ds(half * LANES, LANES), :] = values[0][:, 2 * c + half, :].T

    for copy in to_right:
        copy.wait_recv()
    for copy in to_left:
        copy.start()
    for copy in to_left:
        copy.wait_recv()
    from_left = (lane < COMP * WIN) & (lane % WIN < 8)
    from_right = (lane >= COMP * WIN) & (lane % WIN >= 8)
    level_ref[...] = jnp.where(
        from_left, near_level[0, 0], jnp.where(from_right, near_level[1, 0], own)
    )
    for copy in to_right + to_left:
        copy.wait_send()


def ends_kernel(ob, win, level_ref, out_ref, wout, *rest):
    values, details = rest[: LEVELS + 1], rest[LEVELS + 1 : 2 * LEVELS + 1]
    (out_sem,) = rest[2 * LEVELS + 1 :]
    rows = out_ref.shape[0]
    stores = []
    for c in range(COMP):
        stores.append(
            pltpu.make_async_copy(
                ob.at[c, pl.ds(HALO, rows - 2 * HALO), :],
                out_ref.at[pl.ds(HALO, rows - 2 * HALO), c, :],
                out_sem.at[c],
            )
        )
        stores[-1].start()
    lane, sublane = lanes_and_sublanes()
    values[0][:, 0, :] = win[...].T
    transform(values, details, lane, level_ref[...], before_in_window, after_in_window)
    wout[...] = values[0][:, 0, :].T
    for c in range(COMP):
        stores.append(
            pltpu.make_async_copy(
                wout.at[pl.ds(c * WIN + 8, HALO), :],
                out_ref.at[pl.ds(0, HALO), c, :],
                out_sem.at[COMP + c],
            )
        )
        stores[-1].start()
        stores.append(
            pltpu.make_async_copy(
                wout.at[pl.ds((COMP + c) * WIN + 8 - HALO, HALO), :],
                out_ref.at[pl.ds(rows - HALO, HALO), c, :],
                out_sem.at[2 * COMP + c],
            )
        )
        stores[-1].start()
    for copy in stores:
        copy.wait()


def lifting_scratch():
    f32 = jnp.float32
    return [pltpu.VMEM((LANES >> level, 8, LANES), f32) for level in range(LEVELS + 1)] + [
        pltpu.VMEM(((LANES >> level) // 2, 8, LANES), f32) for level in range(LEVELS)
    ]


def per_device(sizes, velocity, refine):
    rows = velocity.shape[1] // LANES
    x = velocity.reshape(COMP, rows, LANES).transpose(1, 0, 2)
    x = pltpu.with_memory_space_constraint(x, pltpu.HBM)
    f32 = jnp.float32
    vmem = pl.BlockSpec(memory_space=pltpu.VMEM)
    ob, win, level_of = pl.pallas_call(
        functools.partial(exchange_kernel, sizes),
        out_shape=[
            jax.ShapeDtypeStruct((COMP, rows, LANES), f32),
            jax.ShapeDtypeStruct((LANES, LANES), f32),
            jax.ShapeDtypeStruct((8, LANES), jnp.int32),
        ],
        in_specs=[pl.BlockSpec(memory_space=pltpu.HBM)] * 2,
        out_specs=[vmem] * 3,
        scratch_shapes=[
            pltpu.VMEM((COMP, rows, LANES), f32),
            pltpu.SMEM((1,), jnp.int32),
            pltpu.SMEM((2, 1), jnp.int32),
        ]
        + lifting_scratch()
        + [
            pltpu.SemaphoreType.DMA((COMP,)),
            pltpu.SemaphoreType.DMA((2 * COMP,)),
            pltpu.SemaphoreType.DMA,
            pltpu.SemaphoreType.DMA((2 * COMP + 2,)),
            pltpu.SemaphoreType.DMA((2 * COMP + 2,)),
        ],
        compiler_params=pltpu.CompilerParams(
            collective_id=0, has_side_effects=True, vmem_limit_bytes=VMEM_LIMIT
        ),
    )(x, refine)
    out = pl.pallas_call(
        ends_kernel,
        out_shape=jax.ShapeDtypeStruct(x.shape, f32),
        in_specs=[vmem] * 3,
        out_specs=pl.BlockSpec(memory_space=pltpu.HBM),
        scratch_shapes=[pltpu.VMEM((LANES, LANES), f32)]
        + lifting_scratch()
        + [pltpu.SemaphoreType.DMA((3 * COMP,))],
        compiler_params=pltpu.CompilerParams(vmem_limit_bytes=VMEM_LIMIT),
    )(ob, win, level_of)
    return out.transpose(1, 0, 2).reshape(velocity.shape)


def solution(mesh):
    sizes = tuple(mesh.shape[name] for name in AXES)
    return jax.shard_map(
        functools.partial(per_device, sizes),
        mesh=mesh,
        in_specs=(P(None, AXES), P(AXES)),
        out_specs=P(None, AXES),
        check_vma=False,
    )
```

time: 17.9 us -> 14.8 us (0.83)
  the two profiles are of different devices: /device:TPU:1 before, /device:TPU:0 now
where the time goes in v2:
time: 14.8 us; the launch traced here: 14.6 us
  Pallas kernels  14 us (95%)
  between operations  0.66 us (4%)
    pallas_call x1, Pallas kernels, per_device(): pl.pallas_call(functools.partial(exchange_kernel, sizes), out_shape=[jax....  11.8 us
    pallas_call x1, Pallas kernels, per_device(): pl.pallas_call(ends_kernel, out_shape=jax.ShapeDtypeStruct(x.shape, f32),...  2.15 us

profile of v2, /device:TPU:0, one launch (start us, length us, event | category | flops | bytes accessed | tf_op | source)
XLA Modules:
  0.0 14.6 jit_solution(2243038077334862783)
XLA Ops:
  0.7 11.8 %shard_map.28 = (f32[3,256,128]{2,1,0:T(8,128)S(1)}, f32[128,128]{1,0:T(8,128)S(1)}, s32[8,128]{1,0:T(8,128)S(1)}) custom-call(f32[256,3,128]{2,1,0:T(4,128)} %bitcast.6, s32[1]{0:T(128)S(6)} %copy.3.refine_ref), custom_call_target="tpu_custom_call" | custom-call | tf_op jit(solution)/shard_map/pallas_call | solution.py:275
  12.5 2.2 %shard_map.29 = f32[256,3,128]{2,1,0:T(4,128)} custom-call(f32[3,256,128]{2,1,0:T(8,128)S(1)} %get-tuple-element.8.ob, f32[128,128]{1,0:T(8,128)S(1)} %get-tuple-element.9.win, s32[8,128]{1,0:T(8,128)S(1)} %get-tuple-element.10.level_ref), custom_call_target="tpu_custom_call" | custom-call | tf_op jit(solution)/shard_map/pallas_call | solution.py:301

commit v3 on v2

--- a/solution.py
+++ b/solution.py
@@ -132,7 +132,7 @@
 
 def exchange_kernel(sizes, x_ref, refine_ref, ob, win, level_ref, xb, own_level, near_level, *rest):
     values, details = rest[: LEVELS + 1], rest[LEVELS + 1 : 2 * LEVELS + 1]
-    in_sem, win_sem, level_sem, send_sem, recv_sem = rest[2 * LEVELS + 1 :]
+    in_sem, win_sem, level_sem, send_sem, recv_sem, here_sem = rest[2 * LEVELS + 1 :]
     rows = x_ref.shape[0]
     left, right = neighbours(sizes)
     barrier = pltpu.get_barrier_semaphore()
@@ -188,6 +188,7 @@
             )
         )
     pl.semaphore_wait(barrier, 1)
+    pl.semaphore_signal(here_sem, inc=1, device_id=right, device_id_type=MESH)
     for copy in to_right:
         copy.start()
     for copy in loads + ends:
@@ -205,11 +206,10 @@
         for half in range(2):
             ob[c, pl.ds(half * LANES, LANES), :] = values[0][:, 2 * c + half, :].T
 
-    for copy in to_right:
-        copy.wait_recv()
+    pl.semaphore_wait(here_sem, 1)
     for copy in to_left:
         copy.start()
-    for copy in to_left:
+    for copy in to_right + to_left:
         copy.wait_recv()
     from_left = (lane < COMP * WIN) & (lane % WIN < 8)
     from_right = (lane >= COMP * WIN) & (lane % WIN >= 8)
@@ -293,6 +293,7 @@
             pltpu.SemaphoreType.DMA,
             pltpu.SemaphoreType.DMA((2 * COMP + 2,)),
             pltpu.SemaphoreType.DMA((2 * COMP + 2,)),
+            pltpu.SemaphoreType.REGULAR,
         ],
         compiler_params=pltpu.CompilerParams(
             collective_id=0, has_side_effects=True, vmem_limit_bytes=VMEM_LIMIT

time: 14.8 us -> 13.3 us (0.90)
  Pallas kernels: 14 us -> 12.5 us
    pallas_call x1, Pallas kernels: 11.8 us -> 10.3 us  [per_device(): pl.pallas_call(functools.partial(exchange_kernel, sizes), out_shape=[jax....]
where the time goes in v3:
time: 13.3 us; the launch traced here: 13.2 us
  Pallas kernels  12.5 us (94%)
  between operations  0.66 us (5%)
    pallas_call x1, Pallas kernels, per_device(): pl.pallas_call(functools.partial(exchange_kernel, sizes), out_shape=[jax....  10.3 us
    pallas_call x1, Pallas kernels, per_device(): pl.pallas_call(ends_kernel, out_shape=jax.ShapeDtypeStruct(x.shape, f32),...  2.15 us

profile of v3, /device:TPU:0, one launch (start us, length us, event | category | flops | bytes accessed | tf_op | source)
XLA Modules:
  0.0 13.2 jit_solution(3781863500604409591)
XLA Ops:
  0.7 10.3 %shard_map.28 = (f32[3,256,128]{2,1,0:T(8,128)S(1)}, f32[128,128]{1,0:T(8,128)S(1)}, s32[8,128]{1,0:T(8,128)S(1)}) custom-call(f32[256,3,128]{2,1,0:T(4,128)} %bitcast.6, s32[1]{0:T(128)S(6)} %copy.3.refine_ref), custom_call_target="tpu_custom_call" | custom-call | tf_op jit(solution)/shard_map/pallas_call | solution.py:275
  11.0 2.2 %shard_map.29 = f32[256,3,128]{2,1,0:T(4,128)} custom-call(f32[3,256,128]{2,1,0:T(8,128)S(1)} %get-tuple-element.8.ob, f32[128,128]{1,0:T(8,128)S(1)} %get-tuple-element.9.win, s32[8,128]{1,0:T(8,128)S(1)} %get-tuple-element.10.level_ref), custom_call_target="tpu_custom_call" | custom-call | tf_op jit(solution)/shard_map/pallas_call | solution.py:302

commit v4 on v3

--- a/solution.py
+++ b/solution.py
@@ -28,9 +28,15 @@
     total = nodes * ranks * chips
     me = (lax.axis_index("node") * ranks + lax.axis_index("rank")) * chips + lax.axis_index("chip")
     return (
+        me,
         coordinates(lax.rem(me + total - 1, total), sizes),
         coordinates(lax.rem(me + 1, total), sizes),
     )
+
+
+def on_seam(device, sizes):
+    place = lax.rem(device, sizes[1] * sizes[2])
+    return (place == 0) | (place == sizes[1] * sizes[2] - 1)
 
 
 def after_with_carry(row, lane):
@@ -43,14 +49,6 @@
     rolled = pltpu.roll(row, 1, 1)
     carried = pltpu.roll(rolled, 1, 0)
     return jnp.where(lane == 0, carried, rolled)
-
-
-def after_in_window(row, lane):
-    return pltpu.roll(row, LANES - 1, 1)
-
-
-def before_in_window(row, lane):
-    return pltpu.roll(row, 1, 1)
 
 
 def predict(e):
@@ -130,13 +128,106 @@
     )
 
 
+PARTS = 8
+PART = LANES // PARTS
+
+
+def shifted(value, by, sublane):
+    if by == 0:
+        return value
+    if by > 0:
+        turned = pltpu.roll(value, LANES - 1, 1)
+        if by == PARTS:
+            return turned
+        return pltpu.roll(jnp.where(sublane < by, turned, value), PARTS - by, 0)
+    turned = pltpu.roll(value, 1, 1)
+    if by == -PARTS:
+        return turned
+    return pltpu.roll(jnp.where(sublane >= PARTS + by, turned, value), -by, 0)
+
+
+class Line:
+    def __init__(self, values, sublane):
+        self.values, self.sublane, self.seen = values, sublane, {}
+
+    def __getitem__(self, place):
+        if place not in self.seen:
+            part, slot = divmod(place, len(self.values))
+            self.seen[place] = shifted(self.values[slot], part, self.sublane)
+        return self.seen[place]
+
+
+def predicted(before, here, after, later):
+    return (here + after) * (9.0 / 16.0) - (before + later) * (1.0 / 16.0)
+
+
+def lift_window(rows_in_parts, level_of, sublane):
+    line = Line(rows_in_parts, sublane)
+    kept = []
+    level = 0
+    while len(line.values) > 1:
+        half = len(line.values) // 2
+        detail = {}
+        for i in range(-1, half):
+            detail[i] = line[2 * i + 1] - predicted(
+                line[2 * i - 2], line[2 * i], line[2 * i + 2], line[2 * i + 4]
+            )
+        scaling = [line[2 * i] + (detail[i - 1] + detail[i]) * 0.25 for i in range(half)]
+        keep = level_of > level
+        kept.append(Line([jnp.where(keep, detail[i], 0.0) for i in range(half)], sublane))
+        line = Line(scaling, sublane)
+        level += 1
+    inner = []
+    for apart in (1, 2):
+        at = lambda place: line[place * apart]
+        detail = at(0) - predicted(at(-3), at(-1), at(1), at(3))
+        left = at(-1) - predicted(at(-4), at(-2), at(0), at(2))
+        right = at(1) - predicted(at(-2), at(0), at(2), at(4))
+        inner.append(Line([jnp.where(level_of > level, detail, 0.0)], sublane))
+        line = Line([at(0) + (left + right) * 0.25], sublane)
+        level += 1
+    for apart in (2, 1):
+        k = inner.pop()
+        at = lambda place: k[place * apart]
+        even = line[0] - (at(-1) + at(1)) * 0.25
+        odd = (
+            at(0) * (23.0 / 32.0)
+            - (at(-2) + at(2)) * (1.0 / 8.0)
+            + (at(-4) + at(4)) * (1.0 / 64.0)
+            + predicted(line[-3 * apart], line[-apart], line[apart], line[3 * apart])
+        )
+        line = Line([jnp.where(sublane % (2 * apart) == 0, even, odd)], sublane)
+    wanted = [range(0, PART)]
+    for _ in kept:
+        low = [n // 2 - 1 if n % 2 else n // 2 for n in wanted[-1]]
+        high = [n // 2 + 2 if n % 2 else n // 2 for n in wanted[-1]]
+        wanted.append(range(min(low), max(high) + 1))
+    current = {place: line[place] for place in wanted.pop()}
+    while kept:
+        k = kept.pop()
+        even = {i: value - (k[i - 1] + k[i]) * 0.25 for i, value in current.items()}
+        current = {}
+        for n in wanted.pop():
+            i = n // 2
+            if n % 2:
+                current[n] = k[i] + predicted(even[i - 1], even[i], even[i + 1], even[i + 2])
+            else:
+                current[n] = even[i]
+    return [current[n] for n in range(PART)]
+
+
 def exchange_kernel(sizes, x_ref, refine_ref, ob, win, level_ref, xb, own_level, near_level, *rest):
     values, details = rest[: LEVELS + 1], rest[LEVELS + 1 : 2 * LEVELS + 1]
     in_sem, win_sem, level_sem, send_sem, recv_sem, here_sem = rest[2 * LEVELS + 1 :]
     rows = x_ref.shape[0]
-    left, right = neighbours(sizes)
+    me, left, right = neighbours(sizes)
+    left_seam, right_seam = on_seam(me, sizes), on_seam(me + 1, sizes)
     barrier = pltpu.get_barrier_semaphore()
     pl.semaphore_signal(barrier, inc=1, device_id=left, device_id_type=MESH)
+
+    @pl.when(jnp.logical_not(right_seam))
+    def _():
+        pl.semaphore_signal(barrier, inc=1, device_id=right, device_id_type=MESH)
 
     loads = []
     for c in range(COMP):
@@ -187,10 +278,19 @@
                 left,
             )
         )
-    pl.semaphore_wait(barrier, 1)
-    pl.semaphore_signal(here_sem, inc=1, device_id=right, device_id_type=MESH)
+    pl.semaphore_wait(barrier, jnp.where(left_seam, 1, 2))
     for copy in to_right:
         copy.start()
+
+    @pl.when(right_seam)
+    def _():
+        pl.semaphore_signal(here_sem, inc=1, device_id=right, device_id_type=MESH)
+
+    @pl.when(jnp.logical_not(left_seam))
+    def _():
+        for copy in to_left:
+            copy.start()
+
     for copy in loads + ends:
         copy.wait()
 
@@ -206,9 +306,12 @@
         for half in range(2):
             ob[c, pl.ds(half * LANES, LANES), :] = values[0][:, 2 * c + half, :].T
 
-    pl.semaphore_wait(here_sem, 1)
-    for copy in to_left:
-        copy.start()
+    @pl.when(left_seam)
+    def _():
+        pl.semaphore_wait(here_sem, 1)
+        for copy in to_left:
+            copy.start()
+
     for copy in to_right + to_left:
         copy.wait_recv()
     from_left = (lane < COMP * WIN) & (lane % WIN < 8)
@@ -220,9 +323,7 @@
         copy.wait_send()
 
 
-def ends_kernel(ob, win, level_ref, out_ref, wout, *rest):
-    values, details = rest[: LEVELS + 1], rest[LEVELS + 1 : 2 * LEVELS + 1]
-    (out_sem,) = rest[2 * LEVELS + 1 :]
+def ends_kernel(ob, win, level_ref, out_ref, wout, turned, out_sem):
     rows = out_ref.shape[0]
     stores = []
     for c in range(COMP):
@@ -235,9 +336,11 @@
         )
         stores[-1].start()
     lane, sublane = lanes_and_sublanes()
-    values[0][:, 0, :] = win[...].T
-    transform(values, details, lane, level_ref[...], before_in_window, after_in_window)
-    wout[...] = values[0][:, 0, :].T
+    turned[...] = win[...].T
+    parts = [turned[pl.ds(k, PARTS, stride=PART), :] for k in range(PART)]
+    for k, value in enumerate(lift_window(parts, level_ref[...], sublane)):
+        turned[pl.ds(k, PARTS, stride=PART), :] = value
+    wout[...] = turned[...].T
     for c in range(COMP):
         stores.append(
             pltpu.make_async_copy(
@@ -304,8 +407,7 @@
         out_shape=jax.ShapeDtypeStruct(x.shape, f32),
         in_specs=[vmem] * 3,
         out_specs=pl.BlockSpec(memory_space=pltpu.HBM),
-        scratch_shapes=[pltpu.VMEM((LANES, LANES), f32)]
-        + lifting_scratch()
+        scratch_shapes=[pltpu.VMEM((LANES, LANES), f32)] * 2
         + [pltpu.SemaphoreType.DMA((3 * COMP,))],
         compiler_params=pltpu.CompilerParams(vmem_limit_bytes=VMEM_LIMIT),
     )(ob, win, level_of)

time: 13.3 us -> 12.7 us (0.955)
  Pallas kernels: 12.5 us -> 12 us
    pallas_call x1, Pallas kernels: 2.15 us -> 1.61 us  [per_device(): pl.pallas_call(ends_kernel, out_shape=jax.ShapeDtypeStruct(x.shape, f32),...]
where the time goes in v4:
time: 12.7 us; the launch traced here: 12.6 us
  Pallas kernels  12 us (94%)
  between operations  0.66 us (5%)
    pallas_call x1, Pallas kernels, per_device(): pl.pallas_call(functools.partial(exchange_kernel, sizes), out_shape=[jax....  10.4 us
    pallas_call x1, Pallas kernels, per_device(): pl.pallas_call(ends_kernel, out_shape=jax.ShapeDtypeStruct(x.shape, f32),...  1.61 us

profile of v4, /device:TPU:0, one launch (start us, length us, event | category | flops | bytes accessed | tf_op | source)
XLA Modules:
  0.0 12.6 jit_solution(12584547114591551530)
XLA Ops:
  0.7 10.4 %shard_map.28 = (f32[3,256,128]{2,1,0:T(8,128)S(1)}, f32[128,128]{1,0:T(8,128)S(1)}, s32[8,128]{1,0:T(8,128)S(1)}) custom-call(f32[256,3,128]{2,1,0:T(4,128)} %bitcast.6, s32[1]{0:T(128)S(6)} %copy.3.refine_ref), custom_call_target="tpu_custom_call" | custom-call | tf_op jit(solution)/shard_map/pallas_call | solution.py:378
  11.0 1.6 %shard_map.29 = f32[256,3,128]{2,1,0:T(4,128)} custom-call(f32[3,256,128]{2,1,0:T(8,128)S(1)} %get-tuple-element.8.ob, f32[128,128]{1,0:T(8,128)S(1)} %get-tuple-element.9.win, s32[8,128]{1,0:T(8,128)S(1)} %get-tuple-element.10.level_ref), custom_call_target="tpu_custom_call" | custom-call | tf_op jit(solution)/shard_map/pallas_call | solution.py:405

commit v5 on v4

--- a/solution.py
+++ b/solution.py
@@ -13,7 +13,8 @@
 COMP = 3
 MESH = pl.DeviceIdType.MESH
 HALO = 3
-WIN = 16
+WIN = 3 * HALO
+SIDES = 8
 CHUNK = 8
 VMEM_LIMIT = 8 << 20
 
@@ -136,11 +137,11 @@
     if by == 0:
         return value
     if by > 0:
-        turned = pltpu.roll(value, LANES - 1, 1)
+        turned = pltpu.roll(value, LANES - SIDES, 1)
         if by == PARTS:
             return turned
         return pltpu.roll(jnp.where(sublane < by, turned, value), PARTS - by, 0)
-    turned = pltpu.roll(value, 1, 1)
+    turned = pltpu.roll(value, SIDES, 1)
     if by == -PARTS:
         return turned
     return pltpu.roll(jnp.where(sublane >= PARTS + by, turned, value), -by, 0)
@@ -229,26 +230,6 @@
     def _():
         pl.semaphore_signal(barrier, inc=1, device_id=right, device_id_type=MESH)
 
-    loads = []
-    for c in range(COMP):
-        loads.append(pltpu.make_async_copy(x_ref.at[:, c, :], xb.at[c], in_sem.at[c]))
-    ends = [pltpu.make_async_copy(refine_ref, own_level, level_sem)]
-    for c in range(COMP):
-        ends.append(
-            pltpu.make_async_copy(
-                x_ref.at[pl.ds(0, 8), c, :], win.at[pl.ds(c * WIN + 8, 8), :], win_sem.at[c]
-            )
-        )
-        ends.append(
-            pltpu.make_async_copy(
-                x_ref.at[pl.ds(rows - 8, 8), c, :],
-                win.at[pl.ds((COMP + c) * WIN, 8), :],
-                win_sem.at[COMP + c],
-            )
-        )
-    for copy in loads + ends:
-        copy.start()
-
     def remote(src, dst, index, device):
         return pltpu.make_async_remote_copy(
             src_ref=src,
@@ -259,25 +240,15 @@
             device_id_type=MESH,
         )
 
-    to_right = [remote(refine_ref, near_level.at[0], 2 * COMP, right)]
-    to_left = [remote(refine_ref, near_level.at[1], 2 * COMP + 1, left)]
-    for c in range(COMP):
-        to_right.append(
-            remote(
-                x_ref.at[pl.ds(rows - HALO, HALO), c, :],
-                win.at[pl.ds(c * WIN + 8 - HALO, HALO), :],
-                c,
-                right,
-            )
-        )
-        to_left.append(
-            remote(
-                x_ref.at[pl.ds(0, HALO), c, :],
-                win.at[pl.ds((COMP + c) * WIN + 8, HALO), :],
-                COMP + c,
-                left,
-            )
-        )
+    low, high = pl.ds(0, COMP), pl.ds(COMP, COMP)
+    to_right = [
+        remote(x_ref.at[pl.ds(rows - HALO, HALO)], win.at[pl.ds(0, HALO), low, :], 0, right),
+        remote(refine_ref, near_level.at[0], 1, right),
+    ]
+    to_left = [
+        remote(x_ref.at[pl.ds(0, HALO)], win.at[pl.ds(2 * HALO, HALO), high, :], 2, left),
+        remote(refine_ref, near_level.at[1], 3, left),
+    ]
     pl.semaphore_wait(barrier, jnp.where(left_seam, 1, 2))
     for copy in to_right:
         copy.start()
@@ -291,7 +262,20 @@
         for copy in to_left:
             copy.start()
 
-    for copy in loads + ends:
+    loads = [
+        pltpu.make_async_copy(x_ref.at[:, c, :], xb.at[c], in_sem.at[c]) for c in range(COMP)
+    ] + [
+        pltpu.make_async_copy(refine_ref, own_level, level_sem),
+        pltpu.make_async_copy(
+            x_ref.at[pl.ds(0, 2 * HALO)], win.at[pl.ds(HALO, 2 * HALO), low, :], win_sem.at[0]
+        ),
+        pltpu.make_async_copy(
+            x_ref.at[pl.ds(rows - 2 * HALO, 2 * HALO)], win.at[pl.ds(0, 2 * HALO), high, :], win_sem.at[1]
+        ),
+    ]
+    for copy in loads:
+        copy.start()
+    for copy in loads:
         copy.wait()
 
     lane, sublane = lanes_and_sublanes()
@@ -313,14 +297,15 @@
             copy.start()
 
     for copy in to_right + to_left:
+        copy.wait_send()
+    for copy in to_right + to_left:
         copy.wait_recv()
-    from_left = (lane < COMP * WIN) & (lane % WIN < 8)
-    from_right = (lane >= COMP * WIN) & (lane % WIN >= 8)
+    side, row = lane % SIDES, lane // SIDES
+    from_left = (side < COMP) & (row < HALO)
+    from_right = (side >= COMP) & (row >= 2 * HALO)
     level_ref[...] = jnp.where(
         from_left, near_level[0, 0], jnp.where(from_right, near_level[1, 0], own)
     )
-    for copy in to_right + to_left:
-        copy.wait_send()
 
 
 def ends_kernel(ob, win, level_ref, out_ref, wout, turned, out_sem):
@@ -336,25 +321,17 @@
         )
         stores[-1].start()
     lane, sublane = lanes_and_sublanes()
-    turned[...] = win[...].T
+    used = WIN * SIDES
+    turned[:, :used] = win[...].reshape(used, LANES).T
     parts = [turned[pl.ds(k, PARTS, stride=PART), :] for k in range(PART)]
     for k, value in enumerate(lift_window(parts, level_ref[...], sublane)):
         turned[pl.ds(k, PARTS, stride=PART), :] = value
-    wout[...] = turned[...].T
-    for c in range(COMP):
+    redone = turned[...].T[HALO * SIDES : 2 * HALO * SIDES]
+    wout[...] = redone.reshape(HALO, SIDES, LANES)
+    for side, first in ((0, 0), (1, rows - HALO)):
         stores.append(
             pltpu.make_async_copy(
-                wout.at[pl.ds(c * WIN + 8, HALO), :],
-                out_ref.at[pl.ds(0, HALO), c, :],
-                out_sem.at[COMP + c],
-            )
-        )
-        stores[-1].start()
-        stores.append(
-            pltpu.make_async_copy(
-                wout.at[pl.ds((COMP + c) * WIN + 8 - HALO, HALO), :],
-                out_ref.at[pl.ds(rows - HALO, HALO), c, :],
-                out_sem.at[2 * COMP + c],
+                wout.at[:, pl.ds(side * COMP, COMP), :], out_ref.at[pl.ds(first, HALO)], out_sem.at[COMP + side]
             )
         )
         stores[-1].start()
@@ -379,7 +356,7 @@
         functools.partial(exchange_kernel, sizes),
         out_shape=[
             jax.ShapeDtypeStruct((COMP, rows, LANES), f32),
-            jax.ShapeDtypeStruct((LANES, LANES), f32),
+            jax.ShapeDtypeStruct((WIN, SIDES, LANES), f32),
             jax.ShapeDtypeStruct((8, LANES), jnp.int32),
         ],
         in_specs=[pl.BlockSpec(memory_space=pltpu.HBM)] * 2,
@@ -392,10 +369,10 @@
         + lifting_scratch()
         + [
             pltpu.SemaphoreType.DMA((COMP,)),
-            pltpu.SemaphoreType.DMA((2 * COMP,)),
+            pltpu.SemaphoreType.DMA((2,)),
             pltpu.SemaphoreType.DMA,
-            pltpu.SemaphoreType.DMA((2 * COMP + 2,)),
-            pltpu.SemaphoreType.DMA((2 * COMP + 2,)),
+            pltpu.SemaphoreType.DMA((4,)),
+            pltpu.SemaphoreType.DMA((4,)),
             pltpu.SemaphoreType.REGULAR,
         ],
         compiler_params=pltpu.CompilerParams(
@@ -407,8 +384,11 @@
         out_shape=jax.ShapeDtypeStruct(x.shape, f32),
         in_specs=[vmem] * 3,
         out_specs=pl.BlockSpec(memory_space=pltpu.HBM),
-        scratch_shapes=[pltpu.VMEM((LANES, LANES), f32)] * 2
-        + [pltpu.SemaphoreType.DMA((3 * COMP,))],
+        scratch_shapes=[
+            pltpu.VMEM((HALO, SIDES, LANES), f32),
+            pltpu.VMEM((LANES, LANES), f32),
+            pltpu.SemaphoreType.DMA((COMP + 2,)),
+        ],
         compiler_params=pltpu.CompilerParams(vmem_limit_bytes=VMEM_LIMIT),
     )(ob, win, level_of)
     return out.transpose(1, 0, 2).reshape(velocity.shape)

time: 12.7 us -> 12.6 us (level)
  no operation moved by 1% of the time
where the time goes in v5:
time: 12.6 us; the launch traced here: 12.5 us
  Pallas kernels  11.9 us (94%)
  between operations  0.66 us (5%)
    pallas_call x1, Pallas kernels, per_device(): pl.pallas_call(functools.partial(exchange_kernel, sizes), out_shape=[jax....  10.3 us
    pallas_call x1, Pallas kernels, per_device(): pl.pallas_call(ends_kernel, out_shape=jax.ShapeDtypeStruct(x.shape, f32),...  1.57 us

profile of v5, /device:TPU:0, one launch (start us, length us, event | category | flops | bytes accessed | tf_op | source)
XLA Modules:
  0.0 12.5 jit_solution(2384986402449858025)
XLA Ops:
  0.7 10.3 %shard_map.28 = (f32[3,256,128]{2,1,0:T(8,128)S(1)}, f32[9,8,128]{2,1,0:T(8,128)S(1)}, s32[8,128]{1,0:T(8,128)S(1)}) custom-call(f32[256,3,128]{2,1,0:T(4,128)} %bitcast.6, s32[1]{0:T(128)S(6)} %copy.3.refine_ref), custom_call_target="tpu_custom_call" | custom-call | tf_op jit(solution)/shard_map/pallas_call | solution.py:355
  10.9 1.6 %shard_map.29 = f32[256,3,128]{2,1,0:T(4,128)} custom-call(f32[3,256,128]{2,1,0:T(8,128)S(1)} %get-tuple-element.8.ob, f32[9,8,128]{2,1,0:T(8,128)S(1)} %get-tuple-element.9.win, s32[8,128]{1,0:T(8,128)S(1)} %get-tuple-element.10.level_ref), custom_call_target="tpu_custom_call" | custom-call | tf_op jit(solution)/shard_map/pallas_call | solution.py:382

commit v6 on v5

--- a/solution.py
+++ b/solution.py
@@ -133,77 +133,114 @@
 PART = LANES // PARTS
 
 
-def shifted(value, by, sublane):
-    if by == 0:
-        return value
-    if by > 0:
-        turned = pltpu.roll(value, LANES - SIDES, 1)
-        if by == PARTS:
-            return turned
-        return pltpu.roll(jnp.where(sublane < by, turned, value), PARTS - by, 0)
-    turned = pltpu.roll(value, SIDES, 1)
-    if by == -PARTS:
-        return turned
-    return pltpu.roll(jnp.where(sublane >= PARTS + by, turned, value), -by, 0)
-
-
-class Line:
+def rows_away(value, by):
+    return pltpu.roll(value, (-by * SIDES) % LANES, 1) if by else value
+
+
+def parts_away(here, beyond, by, sublane):
+    turn = (-by) % PARTS
+    inside = sublane < PARTS - by if by > 0 else sublane >= -by
+    return jnp.where(inside, pltpu.roll(here, turn, 0), pltpu.roll(beyond, turn, 0))
+
+
+def predicted(before, here, after, later):
+    return (here + after) * (9.0 / 16.0) - (before + later) * (1.0 / 16.0)
+
+
+def by_place(values, beyond, place, sublane):
+    part, slot = divmod(place, len(values))
+    if part == 0:
+        return values[slot]
+    return parts_away(values[slot], beyond[slot], part, sublane)
+
+
+class Rows:
+    def __init__(self, values, sublane):
+        self.values, self.sublane = values, sublane
+
+    def at(self, row, by):
+        away, by = (row + by // PARTS, 0) if by % PARTS == 0 else (row, by)
+        if by == 0:
+            return self.values[away]
+        beyond = self.values.get(away + (1 if by > 0 else -1), self.values[away])
+        return parts_away(self.values[away], beyond, by, self.sublane)
+
+
+class Kept:
     def __init__(self, values, sublane):
         self.values, self.sublane, self.seen = values, sublane, {}
 
     def __getitem__(self, place):
         if place not in self.seen:
             part, slot = divmod(place, len(self.values))
-            self.seen[place] = shifted(self.values[slot], part, self.sublane)
+            value = self.values[slot]
+            if part:
+                beyond = rows_away(value, 1 if part > 0 else -1)
+                value = parts_away(value, beyond, part, self.sublane)
+            self.seen[place] = value
         return self.seen[place]
 
 
-def predicted(before, here, after, later):
-    return (here + after) * (9.0 / 16.0) - (before + later) * (1.0 / 16.0)
-
-
-def lift_window(rows_in_parts, level_of, sublane):
-    line = Line(rows_in_parts, sublane)
+def lift_window(inner, outer, level_of, sublane):
     kept = []
     level = 0
-    while len(line.values) > 1:
-        half = len(line.values) // 2
-        detail = {}
-        for i in range(-1, half):
-            detail[i] = line[2 * i + 1] - predicted(
-                line[2 * i - 2], line[2 * i], line[2 * i + 2], line[2 * i + 4]
+    while len(inner) > 1:
+        half = len(inner) // 2
+        halves = []
+        for mine, other in ((inner, outer), (outer, inner)):
+            at = lambda place: by_place(mine, other, place, sublane)
+            ahead = [at(2 * i) for i in range(-2, half + 2)]
+            detail = [
+                at(2 * i + 1) - predicted(*ahead[i + 1 : i + 5]) for i in range(-1, half)
+            ]
+            scaling = [
+                ahead[i + 2] + (detail[i] + detail[i + 1]) * 0.25 for i in range(half)
+            ]
+            halves.append((detail[1:], scaling))
+        kept.append(Kept([jnp.where(level_of > level, d, 0.0) for d in halves[0][0]], sublane))
+        inner, outer = halves[0][1], halves[1][1]
+        level += 1
+    levels = {row: rows_away(level_of, row) for row in range(-2, 3)}
+    line = Rows({row: rows_away(inner[0], row) for row in range(-4, 5)}, sublane)
+    inside = []
+    for apart, reach, held in ((1, 3, 1), (2, 2, 2)):
+        scaling = {}
+        for row in range(-reach, reach + 1):
+            at = lambda by: line.at(row, by * apart)
+            scaling[row] = (
+                at(0) * (23.0 / 32.0)
+                + (at(-1) + at(1)) * 0.25
+                - (at(-2) + at(2)) * 0.125
+                + (at(-4) + at(4)) * (1.0 / 64.0)
             )
-        scaling = [line[2 * i] + (detail[i - 1] + detail[i]) * 0.25 for i in range(half)]
-        keep = level_of > level
-        kept.append(Line([jnp.where(keep, detail[i], 0.0) for i in range(half)], sublane))
-        line = Line(scaling, sublane)
-        level += 1
-    inner = []
-    for apart in (1, 2):
-        at = lambda place: line[place * apart]
-        detail = at(0) - predicted(at(-3), at(-1), at(1), at(3))
-        left = at(-1) - predicted(at(-4), at(-2), at(0), at(2))
-        right = at(1) - predicted(at(-2), at(0), at(2), at(4))
-        inner.append(Line([jnp.where(level_of > level, detail, 0.0)], sublane))
-        line = Line([at(0) + (left + right) * 0.25], sublane)
+        details = {}
+        for row in range(-held, held + 1):
+            at = lambda by: line.at(row, by * apart)
+            detail = at(0) - predicted(at(-3), at(-1), at(1), at(3))
+            details[row] = jnp.where(levels[row] > level, detail, 0.0)
+        inside.append(Rows(details, sublane))
+        line = Rows(scaling, sublane)
         level += 1
     for apart in (2, 1):
-        k = inner.pop()
-        at = lambda place: k[place * apart]
-        even = line[0] - (at(-1) + at(1)) * 0.25
-        odd = (
-            at(0) * (23.0 / 32.0)
-            - (at(-2) + at(2)) * (1.0 / 8.0)
-            + (at(-4) + at(4)) * (1.0 / 64.0)
-            + predicted(line[-3 * apart], line[-apart], line[apart], line[3 * apart])
-        )
-        line = Line([jnp.where(sublane % (2 * apart) == 0, even, odd)], sublane)
+        k = inside.pop()
+        values = {}
+        for row in (-1, 0, 1):
+            at = lambda by: k.at(row, by * apart)
+            even = line.at(row, 0) - (at(-1) + at(1)) * 0.25
+            odd = (
+                at(0) * (23.0 / 32.0)
+                - (at(-2) + at(2)) * 0.125
+                + (at(-4) + at(4)) * (1.0 / 64.0)
+                + predicted(*(line.at(row, by * apart) for by in (-3, -1, 1, 3)))
+            )
+            values[row] = jnp.where(sublane % (2 * apart) == 0, even, odd)
+        line = Rows(values, sublane)
     wanted = [range(0, PART)]
     for _ in kept:
         low = [n // 2 - 1 if n % 2 else n // 2 for n in wanted[-1]]
         high = [n // 2 + 2 if n % 2 else n // 2 for n in wanted[-1]]
         wanted.append(range(min(low), max(high) + 1))
-    current = {place: line[place] for place in wanted.pop()}
+    current = {place: line.at(0, place) for place in wanted.pop()}
     while kept:
         k = kept.pop()
         even = {i: value - (k[i - 1] + k[i]) * 0.25 for i, value in current.items()}
@@ -308,7 +345,7 @@
     )
 
 
-def ends_kernel(ob, win, level_ref, out_ref, wout, turned, out_sem):
+def ends_kernel(ob, win, level_ref, out_ref, wout, turned, beyond, out_sem):
     rows = out_ref.shape[0]
     stores = []
     for c in range(COMP):
@@ -322,9 +359,16 @@
         stores[-1].start()
     lane, sublane = lanes_and_sublanes()
     used = WIN * SIDES
-    turned[:, :used] = win[...].reshape(used, LANES).T
-    parts = [turned[pl.ds(k, PARTS, stride=PART), :] for k in range(PART)]
-    for k, value in enumerate(lift_window(parts, level_ref[...], sublane)):
+    rows_here = win[...]
+    rows_next = jnp.concatenate([rows_here[1:], rows_here[:1]], axis=0)
+    rows_last = jnp.concatenate([rows_here[WIN - 1 :], rows_here[: WIN - 1]], axis=0)
+    cell = lax.broadcasted_iota(jnp.int32, rows_here.shape, 2)
+    around = jnp.where(cell < LANES // 2, rows_next, rows_last)
+    turned[:, :used] = rows_here.reshape(used, LANES).T
+    beyond[:, :used] = around.reshape(used, LANES).T
+    inner = [turned[pl.ds(k, PARTS, stride=PART), :] for k in range(PART)]
+    outer = [beyond[pl.ds(k, PARTS, stride=PART), :] for k in range(PART)]
+    for k, value in enumerate(lift_window(inner, outer, level_ref[...], sublane)):
         turned[pl.ds(k, PARTS, stride=PART), :] = value
     redone = turned[...].T[HALO * SIDES : 2 * HALO * SIDES]
     wout[...] = redone.reshape(HALO, SIDES, LANES)
@@ -387,6 +431,7 @@
         scratch_shapes=[
             pltpu.VMEM((HALO, SIDES, LANES), f32),
             pltpu.VMEM((LANES, LANES), f32),
+            pltpu.VMEM((LANES, LANES), f32),
             pltpu.SemaphoreType.DMA((COMP + 2,)),
         ],
         compiler_params=pltpu.CompilerParams(vmem_limit_bytes=VMEM_LIMIT),

time: 12.6 us -> 12.1 us (0.960)
  Pallas kernels: 11.9 us -> 11.4 us
    pallas_call x1, Pallas kernels: 1.57 us -> 1.09 us  [per_device(): pl.pallas_call(ends_kernel, out_shape=jax.ShapeDtypeStruct(x.shape, f32),...]
where the time goes in v6:
time: 12.1 us; the launch traced here: 12 us
  Pallas kernels  11.4 us (94%)
  between operations  0.66 us (5%)
    pallas_call x1, Pallas kernels, per_device(): pl.pallas_call(functools.partial(exchange_kernel, sizes), out_shape=[jax....  10.3 us
    pallas_call x1, Pallas kernels, per_device(): pl.pallas_call(ends_kernel, out_shape=jax.ShapeDtypeStruct(x.shape, f32),...  1.09 us

profile of v6, /device:TPU:0, one launch (start us, length us, event | category | flops | bytes accessed | tf_op | source)
XLA Modules:
  0.0 12.0 jit_solution(6483652844414559937)
XLA Ops:
  0.7 10.3 %shard_map.28 = (f32[3,256,128]{2,1,0:T(8,128)S(1)}, f32[9,8,128]{2,1,0:T(8,128)S(1)}, s32[8,128]{1,0:T(8,128)S(1)}) custom-call(f32[256,3,128]{2,1,0:T(4,128)} %bitcast.6, s32[1]{0:T(128)S(6)} %copy.3.refine_ref), custom_call_target="tpu_custom_call" | custom-call | tf_op jit(solution)/shard_map/pallas_call | solution.py:399
  10.9 1.1 %shard_map.29 = f32[256,3,128]{2,1,0:T(4,128)} custom-call(f32[3,256,128]{2,1,0:T(8,128)S(1)} %get-tuple-element.8.ob, f32[9,8,128]{2,1,0:T(8,128)S(1)} %get-tuple-element.9.win, s32[8,128]{1,0:T(8,128)S(1)} %get-tuple-element.10.level_ref), custom_call_target="tpu_custom_call" | custom-call | tf_op jit(solution)/shard_map/pallas_call | solution.py:426

commit v7 on v6

--- a/solution.py
+++ b/solution.py
@@ -19,25 +19,32 @@
 VMEM_LIMIT = 8 << 20
 
 
-def coordinates(flat, sizes):
-    nodes, ranks, chips = sizes
-    return (flat // (ranks * chips), (flat // chips) % ranks, flat % chips)
-
-
 def neighbours(sizes):
     nodes, ranks, chips = sizes
-    total = nodes * ranks * chips
-    me = (lax.axis_index("node") * ranks + lax.axis_index("rank")) * chips + lax.axis_index("chip")
-    return (
-        me,
-        coordinates(lax.rem(me + total - 1, total), sizes),
-        coordinates(lax.rem(me + 1, total), sizes),
-    )
+    node, rank, chip = (lax.axis_index(name) for name in AXES)
+    first_chip, last_chip = chip == 0, chip == chips - 1
+    first, last = first_chip & (rank == 0), last_chip & (rank == ranks - 1)
+    left = (
+        jnp.where(first, jnp.where(node == 0, nodes - 1, node - 1), node),
+        jnp.where(first_chip, jnp.where(rank == 0, ranks - 1, rank - 1), rank),
+        jnp.where(first_chip, chips - 1, chip - 1),
+    )
+    right = (
+        jnp.where(last, jnp.where(node == nodes - 1, 0, node + 1), node),
+        jnp.where(last_chip, jnp.where(rank == ranks - 1, 0, rank + 1), rank),
+        jnp.where(last_chip, 0, chip + 1),
+    )
+    return (node, rank, chip), left, right
 
 
 def on_seam(device, sizes):
-    place = lax.rem(device, sizes[1] * sizes[2])
-    return (place == 0) | (place == sizes[1] * sizes[2] - 1)
+    _, rank, chip = device
+    return ((rank == 0) & (chip == 0)) | ((rank == sizes[1] - 1) & (chip == sizes[2] - 1))
+
+
+def wait_for_rows(count, buffer, semaphore):
+    rows = buffer.at[0, pl.ds(0, count), :]
+    pltpu.make_async_copy(rows, rows, semaphore).wait()
 
 
 def after_with_carry(row, lane):
@@ -254,12 +261,12 @@
     return [current[n] for n in range(PART)]
 
 
-def exchange_kernel(sizes, x_ref, refine_ref, ob, win, level_ref, xb, own_level, near_level, *rest):
+def exchange_kernel(sizes, x_ref, refine_ref, ob, win, level_ref, xb, near_level, *rest):
     values, details = rest[: LEVELS + 1], rest[LEVELS + 1 : 2 * LEVELS + 1]
-    in_sem, win_sem, level_sem, send_sem, recv_sem, here_sem = rest[2 * LEVELS + 1 :]
+    in_sem, send_sem, recv_sem, level_send_sem, level_recv_sem, here_sem = rest[2 * LEVELS + 1 :]
     rows = x_ref.shape[0]
     me, left, right = neighbours(sizes)
-    left_seam, right_seam = on_seam(me, sizes), on_seam(me + 1, sizes)
+    left_seam, right_seam = on_seam(me, sizes), on_seam(right, sizes)
     barrier = pltpu.get_barrier_semaphore()
     pl.semaphore_signal(barrier, inc=1, device_id=left, device_id_type=MESH)
 
@@ -267,24 +274,32 @@
     def _():
         pl.semaphore_signal(barrier, inc=1, device_id=right, device_id_type=MESH)
 
-    def remote(src, dst, index, device):
+    def remote(src, dst, sent, come, device):
         return pltpu.make_async_remote_copy(
             src_ref=src,
             dst_ref=dst,
-            send_sem=send_sem.at[index],
-            recv_sem=recv_sem.at[index],
+            send_sem=sent,
+            recv_sem=come,
             device_id=device,
             device_id_type=MESH,
         )
 
     low, high = pl.ds(0, COMP), pl.ds(COMP, COMP)
+    level_right = remote(
+        refine_ref, near_level.at[0], level_send_sem.at[0], level_recv_sem.at[0], right
+    )
+    level_left = remote(refine_ref, near_level.at[1], level_send_sem.at[1], level_recv_sem.at[1], left)
     to_right = [
-        remote(x_ref.at[pl.ds(rows - HALO, HALO)], win.at[pl.ds(0, HALO), low, :], 0, right),
-        remote(refine_ref, near_level.at[0], 1, right),
+        remote(
+            x_ref.at[pl.ds(rows - HALO, HALO)], win.at[pl.ds(0, HALO), low, :], send_sem, recv_sem, right
+        ),
+        level_right,
     ]
     to_left = [
-        remote(x_ref.at[pl.ds(0, HALO)], win.at[pl.ds(2 * HALO, HALO), high, :], 2, left),
-        remote(refine_ref, near_level.at[1], 3, left),
+        remote(
+            x_ref.at[pl.ds(0, HALO)], win.at[pl.ds(2 * HALO, HALO), high, :], send_sem, recv_sem, left
+        ),
+        level_left,
     ]
     pl.semaphore_wait(barrier, jnp.where(left_seam, 1, 2))
     for copy in to_right:
@@ -299,24 +314,15 @@
         for copy in to_left:
             copy.start()
 
-    loads = [
-        pltpu.make_async_copy(x_ref.at[:, c, :], xb.at[c], in_sem.at[c]) for c in range(COMP)
-    ] + [
-        pltpu.make_async_copy(refine_ref, own_level, level_sem),
-        pltpu.make_async_copy(
-            x_ref.at[pl.ds(0, 2 * HALO)], win.at[pl.ds(HALO, 2 * HALO), low, :], win_sem.at[0]
-        ),
-        pltpu.make_async_copy(
-            x_ref.at[pl.ds(rows - 2 * HALO, 2 * HALO)], win.at[pl.ds(0, 2 * HALO), high, :], win_sem.at[1]
-        ),
-    ]
-    for copy in loads:
-        copy.start()
-    for copy in loads:
-        copy.wait()
+    for c in range(COMP):
+        pltpu.make_async_copy(x_ref.at[:, c, :], xb.at[c], in_sem).start()
+    pltpu.make_async_copy(xb, xb, in_sem).wait()
 
     lane, sublane = lanes_and_sublanes()
-    own = own_level[0]
+    own = refine_ref[0]
+    for c in range(COMP):
+        win[pl.ds(HALO, 2 * HALO), c, :] = xb[c, pl.ds(0, 2 * HALO), :]
+        win[pl.ds(0, 2 * HALO), COMP + c, :] = xb[c, pl.ds(rows - 2 * HALO, 2 * HALO), :]
     for c in range(COMP):
         for half in range(2):
             values[0][:, 2 * c + half, :] = xb[c, pl.ds(half * LANES, LANES), :].T
@@ -333,10 +339,12 @@
         for copy in to_left:
             copy.start()
 
-    for copy in to_right + to_left:
-        copy.wait_send()
-    for copy in to_right + to_left:
-        copy.wait_recv()
+    wait_for_rows(2 * HALO * COMP, xb, send_sem)
+    level_right.wait_send()
+    level_left.wait_send()
+    level_right.wait_recv()
+    level_left.wait_recv()
+    wait_for_rows(2 * HALO * COMP, xb, recv_sem)
     side, row = lane % SIDES, lane // SIDES
     from_left = (side < COMP) & (row < HALO)
     from_right = (side >= COMP) & (row >= 2 * HALO)
@@ -347,16 +355,12 @@
 
 def ends_kernel(ob, win, level_ref, out_ref, wout, turned, beyond, out_sem):
     rows = out_ref.shape[0]
-    stores = []
     for c in range(COMP):
-        stores.append(
-            pltpu.make_async_copy(
-                ob.at[c, pl.ds(HALO, rows - 2 * HALO), :],
-                out_ref.at[pl.ds(HALO, rows - 2 * HALO), c, :],
-                out_sem.at[c],
-            )
-        )
-        stores[-1].start()
+        pltpu.make_async_copy(
+            ob.at[c, pl.ds(HALO, rows - 2 * HALO), :],
+            out_ref.at[pl.ds(HALO, rows - 2 * HALO), c, :],
+            out_sem,
+        ).start()
     lane, sublane = lanes_and_sublanes()
     used = WIN * SIDES
     rows_here = win[...]
@@ -373,14 +377,10 @@
     redone = turned[...].T[HALO * SIDES : 2 * HALO * SIDES]
     wout[...] = redone.reshape(HALO, SIDES, LANES)
     for side, first in ((0, 0), (1, rows - HALO)):
-        stores.append(
-            pltpu.make_async_copy(
-                wout.at[:, pl.ds(side * COMP, COMP), :], out_ref.at[pl.ds(first, HALO)], out_sem.at[COMP + side]
-            )
-        )
-        stores[-1].start()
-    for copy in stores:
-        copy.wait()
+        pltpu.make_async_copy(
+            wout.at[:, pl.ds(side * COMP, COMP), :], out_ref.at[pl.ds(first, HALO)], out_sem
+        ).start()
+    pltpu.make_async_copy(ob, ob, out_sem).wait()
 
 
 def lifting_scratch():
@@ -403,20 +403,19 @@
             jax.ShapeDtypeStruct((WIN, SIDES, LANES), f32),
             jax.ShapeDtypeStruct((8, LANES), jnp.int32),
         ],
-        in_specs=[pl.BlockSpec(memory_space=pltpu.HBM)] * 2,
+        in_specs=[pl.BlockSpec(memory_space=pltpu.HBM), pl.BlockSpec(memory_space=pltpu.SMEM)],
         out_specs=[vmem] * 3,
         scratch_shapes=[
             pltpu.VMEM((COMP, rows, LANES), f32),
-            pltpu.SMEM((1,), jnp.int32),
             pltpu.SMEM((2, 1), jnp.int32),
         ]
         + lifting_scratch()
         + [
-            pltpu.SemaphoreType.DMA((COMP,)),
+            pltpu.SemaphoreType.DMA,
+            pltpu.SemaphoreType.DMA,
+            pltpu.SemaphoreType.DMA,
             pltpu.SemaphoreType.DMA((2,)),
-            pltpu.SemaphoreType.DMA,
-            pltpu.SemaphoreType.DMA((4,)),
-            pltpu.SemaphoreType.DMA((4,)),
+            pltpu.SemaphoreType.DMA((2,)),
             pltpu.SemaphoreType.REGULAR,
         ],
         compiler_params=pltpu.CompilerParams(
@@ -432,7 +431,7 @@
             pltpu.VMEM((HALO, SIDES, LANES), f32),
             pltpu.VMEM((LANES, LANES), f32),
             pltpu.VMEM((LANES, LANES), f32),
-            pltpu.SemaphoreType.DMA((COMP + 2,)),
+            pltpu.SemaphoreType.DMA,
         ],
         compiler_params=pltpu.CompilerParams(vmem_limit_bytes=VMEM_LIMIT),
     )(ob, win, level_of)

time: 12.1 us -> 11.9 us (0.983)
  Pallas kernels: 11.4 us -> 11.2 us
    pallas_call x1, Pallas kernels: 10.3 us -> 10.1 us  [per_device(): pl.pallas_call(functools.partial(exchange_kernel, sizes), out_shape=[jax....]
where the time goes in v7:
time: 11.9 us; the launch traced here: 11.8 us
  Pallas kernels  11.2 us (94%)
  between operations  0.66 us (6%)
    pallas_call x1, Pallas kernels, per_device(): pl.pallas_call(functools.partial(exchange_kernel, sizes), out_shape=[jax....  10.1 us
    pallas_call x1, Pallas kernels, per_device(): pl.pallas_call(ends_kernel, out_shape=jax.ShapeDtypeStruct(x.shape, f32),...  1.05 us

profile of v7, /device:TPU:0, one launch (start us, length us, event | category | flops | bytes accessed | tf_op | source)
XLA Modules:
  0.0 11.8 jit_solution(5275476458177566116)
XLA Ops:
  0.7 10.1 %shard_map.28 = (f32[3,256,128]{2,1,0:T(8,128)S(1)}, f32[9,8,128]{2,1,0:T(8,128)S(1)}, s32[8,128]{1,0:T(8,128)S(1)}) custom-call(f32[256,3,128]{2,1,0:T(4,128)} %bitcast.6, s32[1]{0:T(128)S(6)} %copy.3.refine_ref), custom_call_target="tpu_custom_call" | custom-call | tf_op jit(solution)/shard_map/pallas_call | solution.py:399
  10.8 1.1 %shard_map.29 = f32[256,3,128]{2,1,0:T(4,128)} custom-call(f32[3,256,128]{2,1,0:T(8,128)S(1)} %get-tuple-element.8.ob, f32[9,8,128]{2,1,0:T(8,128)S(1)} %get-tuple-element.9.win, s32[8,128]{1,0:T(8,128)S(1)} %get-tuple-element.10.level_ref), custom_call_target="tpu_custom_call" | custom-call | tf_op jit(solution)/shard_map/pallas_call | solution.py:425

commit v8 on v7

--- a/solution.py
+++ b/solution.py
@@ -138,6 +138,8 @@
 
 PARTS = 8
 PART = LANES // PARTS
+STRIP_ROWS = (72, 24, 16, 16, 16, 16, 40, 16)
+STRIP_FIRST = (-32, -8, -2, -4, -3, -2, -16, -2)
 
 
 def rows_away(value, by):
@@ -154,23 +156,20 @@
     return (here + after) * (9.0 / 16.0) - (before + later) * (1.0 / 16.0)
 
 
-def by_place(values, beyond, place, sublane):
-    part, slot = divmod(place, len(values))
-    if part == 0:
-        return values[slot]
-    return parts_away(values[slot], beyond[slot], part, sublane)
-
-
-class Rows:
-    def __init__(self, values, sublane):
-        self.values, self.sublane = values, sublane
-
-    def at(self, row, by):
-        away, by = (row + by // PARTS, 0) if by % PARTS == 0 else (row, by)
-        if by == 0:
-            return self.values[away]
-        beyond = self.values.get(away + (1 if by > 0 else -1), self.values[away])
-        return parts_away(self.values[away], beyond, by, self.sublane)
+def both_away(pair, by, sublane):
+    here, beyond = pair
+    return parts_away(here, beyond, by, sublane), parts_away(beyond, here, by, sublane)
+
+
+class Strip:
+    def __init__(self, buffer, first):
+        self.buffer, self.first = buffer, first
+
+    def put(self, place, value, apart=1):
+        self.buffer[pl.ds(place - self.first, 8, stride=apart), :] = value
+
+    def get(self, place, apart=1):
+        return self.buffer[pl.ds(place - self.first, 8, stride=apart), :]
 
 
 class Kept:
@@ -188,66 +187,73 @@
         return self.seen[place]
 
 
-def lift_window(inner, outer, level_of, sublane):
+def scaled(before, here, after, twice_before, twice_after):
+    return here * (23.0 / 32.0) - (before + after) * 0.125 + (twice_before + twice_after) * (1.0 / 64.0)
+
+
+def lift_strips(value, level_of, buffers):
+    line, above, evens, kept, kept_above, back, levels, done = (
+        Strip(buffer, first) for buffer, first in zip(buffers, STRIP_FIRST)
+    )
+    for row in range(-3, 4):
+        line.put(row * PARTS, rows_away(value, row))
+    for row in range(-2, 3):
+        levels.put(row * PARTS, rows_away(level_of, row))
+
+    def approached(strip, first):
+        at = lambda by: strip.get(2 * first + by, 2)
+        return scaled(at(-2), at(0), at(2), at(-4), at(4)) + (at(-1) + at(1)) * 0.25
+
+    def detailed(strip, first, level, apart):
+        at = lambda by: strip.get(2 * first + by, 2)
+        detail = at(1) - predicted(at(-2), at(0), at(2), at(4))
+        return jnp.where(levels.get(apart * (2 * first + 1), 2 * apart) > level, detail, 0.0)
+
+    for first in (-8, 0, 8):
+        above.put(first, approached(line, first))
+    for first in (-4, 4):
+        kept.put(first, detailed(line, first, LEVELS - 2, 1))
+    evens.put(-2, approached(above, -2))
+    kept_above.put(-3, detailed(above, -3, LEVELS - 1, 2))
+    for y, k, to in ((evens, kept_above, back), (back, kept, done)):
+        to.put(-2, y.get(-1) - (k.get(-2) + k.get(-1)) * 0.25, 2)
+        to.put(
+            -1,
+            scaled(k.get(-2), k.get(-1), k.get(0), k.get(-3), k.get(1))
+            + predicted(y.get(-2), y.get(-1), y.get(0), y.get(1)),
+            2,
+        )
+    return done
+
+
+def lift_window(inner, outer, level_of, sublane, buffers):
     kept = []
     level = 0
-    while len(inner) > 1:
-        half = len(inner) // 2
-        halves = []
-        for mine, other in ((inner, outer), (outer, inner)):
-            at = lambda place: by_place(mine, other, place, sublane)
-            ahead = [at(2 * i) for i in range(-2, half + 2)]
-            detail = [
-                at(2 * i + 1) - predicted(*ahead[i + 1 : i + 5]) for i in range(-1, half)
-            ]
-            scaling = [
-                ahead[i + 2] + (detail[i] + detail[i + 1]) * 0.25 for i in range(half)
-            ]
-            halves.append((detail[1:], scaling))
-        kept.append(Kept([jnp.where(level_of > level, d, 0.0) for d in halves[0][0]], sublane))
-        inner, outer = halves[0][1], halves[1][1]
+    pairs = list(zip(inner, outer))
+    while len(pairs) > 1:
+        even, odd = pairs[0::2], pairs[1::2]
+        half = len(even)
+        last = both_away(even[-1], -1, sublane)
+        ahead = [last] + even + [
+            both_away(even[i % half], 1 + i // half, sublane) for i in range(2)
+        ]
+        detail = [
+            tuple(odd[i][n] - predicted(*(e[n] for e in ahead[i : i + 4])) for n in (0, 1))
+            for i in range(half)
+        ]
+        back = [both_away(detail[-1], -1, sublane)] + detail
+        pairs = [
+            tuple(even[i][n] + (back[i][n] + back[i + 1][n]) * 0.25 for n in (0, 1)) for i in range(half)
+        ]
+        kept.append(Kept([jnp.where(level_of > level, d[0], 0.0) for d in detail], sublane))
         level += 1
-    levels = {row: rows_away(level_of, row) for row in range(-2, 3)}
-    line = Rows({row: rows_away(inner[0], row) for row in range(-4, 5)}, sublane)
-    inside = []
-    for apart, reach, held in ((1, 3, 1), (2, 2, 2)):
-        scaling = {}
-        for row in range(-reach, reach + 1):
-            at = lambda by: line.at(row, by * apart)
-            scaling[row] = (
-                at(0) * (23.0 / 32.0)
-                + (at(-1) + at(1)) * 0.25
-                - (at(-2) + at(2)) * 0.125
-                + (at(-4) + at(4)) * (1.0 / 64.0)
-            )
-        details = {}
-        for row in range(-held, held + 1):
-            at = lambda by: line.at(row, by * apart)
-            detail = at(0) - predicted(at(-3), at(-1), at(1), at(3))
-            details[row] = jnp.where(levels[row] > level, detail, 0.0)
-        inside.append(Rows(details, sublane))
-        line = Rows(scaling, sublane)
-        level += 1
-    for apart in (2, 1):
-        k = inside.pop()
-        values = {}
-        for row in (-1, 0, 1):
-            at = lambda by: k.at(row, by * apart)
-            even = line.at(row, 0) - (at(-1) + at(1)) * 0.25
-            odd = (
-                at(0) * (23.0 / 32.0)
-                - (at(-2) + at(2)) * 0.125
-                + (at(-4) + at(4)) * (1.0 / 64.0)
-                + predicted(*(line.at(row, by * apart) for by in (-3, -1, 1, 3)))
-            )
-            values[row] = jnp.where(sublane % (2 * apart) == 0, even, odd)
-        line = Rows(values, sublane)
+    done = lift_strips(pairs[0][0], level_of, buffers)
     wanted = [range(0, PART)]
     for _ in kept:
         low = [n // 2 - 1 if n % 2 else n // 2 for n in wanted[-1]]
         high = [n // 2 + 2 if n % 2 else n // 2 for n in wanted[-1]]
         wanted.append(range(min(low), max(high) + 1))
-    current = {place: line.at(0, place) for place in wanted.pop()}
+    current = {place: done.get(place) for place in wanted.pop()}
     while kept:
         k = kept.pop()
         even = {i: value - (k[i - 1] + k[i]) * 0.25 for i, value in current.items()}
@@ -286,9 +292,9 @@
 
     low, high = pl.ds(0, COMP), pl.ds(COMP, COMP)
     level_right = remote(
-        refine_ref, near_level.at[0], level_send_sem.at[0], level_recv_sem.at[0], right
-    )
-    level_left = remote(refine_ref, near_level.at[1], level_send_sem.at[1], level_recv_sem.at[1], left)
+        refine_ref, near_level.at[0], level_send_sem, level_recv_sem, right
+    )
+    level_left = remote(refine_ref, near_level.at[1], level_send_sem, level_recv_sem, left)
     to_right = [
         remote(
             x_ref.at[pl.ds(rows - HALO, HALO)], win.at[pl.ds(0, HALO), low, :], send_sem, recv_sem, right
@@ -340,10 +346,8 @@
             copy.start()
 
     wait_for_rows(2 * HALO * COMP, xb, send_sem)
-    level_right.wait_send()
-    level_left.wait_send()
-    level_right.wait_recv()
-    level_left.wait_recv()
+    for semaphore in (level_send_sem, level_recv_sem):
+        pltpu.make_async_copy(near_level, near_level, semaphore).wait()
     wait_for_rows(2 * HALO * COMP, xb, recv_sem)
     side, row = lane % SIDES, lane // SIDES
     from_left = (side < COMP) & (row < HALO)
@@ -353,7 +357,7 @@
     )
 
 
-def ends_kernel(ob, win, level_ref, out_ref, wout, turned, beyond, out_sem):
+def ends_kernel(ob, win, level_ref, out_ref, wout, turned, beyond, out_sem, *strips):
     rows = out_ref.shape[0]
     for c in range(COMP):
         pltpu.make_async_copy(
@@ -372,7 +376,7 @@
     beyond[:, :used] = around.reshape(used, LANES).T
     inner = [turned[pl.ds(k, PARTS, stride=PART), :] for k in range(PART)]
     outer = [beyond[pl.ds(k, PARTS, stride=PART), :] for k in range(PART)]
-    for k, value in enumerate(lift_window(inner, outer, level_ref[...], sublane)):
+    for k, value in enumerate(lift_window(inner, outer, level_ref[...], sublane, strips)):
         turned[pl.ds(k, PARTS, stride=PART), :] = value
     redone = turned[...].T[HALO * SIDES : 2 * HALO * SIDES]
     wout[...] = redone.reshape(HALO, SIDES, LANES)
@@ -414,8 +418,8 @@
             pltpu.SemaphoreType.DMA,
             pltpu.SemaphoreType.DMA,
             pltpu.SemaphoreType.DMA,
-            pltpu.SemaphoreType.DMA((2,)),
-            pltpu.SemaphoreType.DMA((2,)),
+            pltpu.SemaphoreType.DMA,
+            pltpu.SemaphoreType.DMA,
             pltpu.SemaphoreType.REGULAR,
         ],
         compiler_params=pltpu.CompilerParams(
@@ -432,6 +436,10 @@
             pltpu.VMEM((LANES, LANES), f32),
             pltpu.VMEM((LANES, LANES), f32),
             pltpu.SemaphoreType.DMA,
+        ]
+        + [
+            pltpu.VMEM((count, LANES), jnp.int32 if first == -16 else f32)
+            for count, first in zip(STRIP_ROWS, STRIP_FIRST)
         ],
         compiler_params=pltpu.CompilerParams(vmem_limit_bytes=VMEM_LIMIT),
     )(ob, win, level_of)

time: 11.9 us -> 11.9 us (level)
  no operation moved by 1% of the time
where the time goes in v8:
time: 11.9 us; the launch traced here: 11.8 us
  Pallas kernels  11.1 us (93%)
  between operations  0.66 us (6%)
    pallas_call x1, Pallas kernels, per_device(): pl.pallas_call(functools.partial(exchange_kernel, sizes), out_shape=[jax....  10.1 us
    pallas_call x1, Pallas kernels, per_device(): pl.pallas_call(ends_kernel, out_shape=jax.ShapeDtypeStruct(x.shape, f32),...  1.03 us

profile of v8, /device:TPU:0, one launch (start us, length us, event | category | flops | bytes accessed | tf_op | source)
XLA Modules:
  0.0 11.8 jit_solution(11280695800280334083)
XLA Ops:
  0.7 10.1 %shard_map.28 = (f32[3,256,128]{2,1,0:T(8,128)S(1)}, f32[9,8,128]{2,1,0:T(8,128)S(1)}, s32[8,128]{1,0:T(8,128)S(1)}) custom-call(f32[256,3,128]{2,1,0:T(4,128)} %bitcast.6, s32[1]{0:T(128)S(6)} %copy.3.refine_ref), custom_call_target="tpu_custom_call" | custom-call | tf_op jit(solution)/shard_map/pallas_call | solution.py:403
  10.7 1.0 %shard_map.29 = f32[256,3,128]{2,1,0:T(4,128)} custom-call(f32[3,256,128]{2,1,0:T(8,128)S(1)} %get-tuple-element.8.ob, f32[9,8,128]{2,1,0:T(8,128)S(1)} %get-tuple-element.9.win, s32[8,128]{1,0:T(8,128)S(1)} %get-tuple-element.10.level_ref), custom_call_target="tpu_custom_call" | custom-call | tf_op jit(solution)/shard_map/pallas_call | solution.py:429

commit v9 on v8

--- a/solution.py
+++ b/solution.py
@@ -342,8 +342,15 @@
     @pl.when(left_seam)
     def _():
         pl.semaphore_wait(here_sem, 1)
-        for copy in to_left:
-            copy.start()
+        for c in range(COMP):
+            remote(
+                xb.at[c, pl.ds(0, HALO), :],
+                win.at[pl.ds(2 * HALO, HALO), COMP + c, :],
+                send_sem,
+                recv_sem,
+                left,
+            ).start()
+        level_left.start()
 
     wait_for_rows(2 * HALO * COMP, xb, send_sem)
     for semaphore in (level_send_sem, level_recv_sem):

time: 11.9 us -> 11.8 us (level)
  no operation moved by 1% of the time
where the time goes in v9:
time: 11.8 us; the launch traced here: 11.7 us
  Pallas kernels  11.1 us (94%)
  between operations  0.66 us (6%)
    pallas_call x1, Pallas kernels, per_device(): pl.pallas_call(functools.partial(exchange_kernel, sizes), out_shape=[jax....  10 us
    pallas_call x1, Pallas kernels, per_device(): pl.pallas_call(ends_kernel, out_shape=jax.ShapeDtypeStruct(x.shape, f32),...  1.03 us

profile of v9, /device:TPU:0, one launch (start us, length us, event | category | flops | bytes accessed | tf_op | source)
XLA Modules:
  0.0 11.7 jit_solution(15895489437289068224)
XLA Ops:
  0.7 10.0 %shard_map.28 = (f32[3,256,128]{2,1,0:T(8,128)S(1)}, f32[9,8,128]{2,1,0:T(8,128)S(1)}, s32[8,128]{1,0:T(8,128)S(1)}) custom-call(f32[256,3,128]{2,1,0:T(4,128)} %bitcast.6, s32[1]{0:T(128)S(6)} %copy.3.refine_ref), custom_call_target="tpu_custom_call" | custom-call | tf_op jit(solution)/shard_map/pallas_call | solution.py:410
  10.7 1.0 %shard_map.29 = f32[256,3,128]{2,1,0:T(4,128)} custom-call(f32[3,256,128]{2,1,0:T(8,128)S(1)} %get-tuple-element.8.ob, f32[9,8,128]{2,1,0:T(8,128)S(1)} %get-tuple-element.9.win, s32[8,128]{1,0:T(8,128)S(1)} %get-tuple-element.10.level_ref), custom_call_target="tpu_custom_call" | custom-call | tf_op jit(solution)/shard_map/pallas_call | solution.py:436

commit v10 on v9

--- a/solution.py
+++ b/solution.py
@@ -11,7 +11,7 @@
 LEVELS = 6
 LANES = 128
 COMP = 3
-MESH = pl.DeviceIdType.MESH
+LOGICAL = pl.DeviceIdType.LOGICAL
 HALO = 3
 WIN = 3 * HALO
 SIDES = 8
@@ -21,25 +21,15 @@
 
 def neighbours(sizes):
     nodes, ranks, chips = sizes
+    total = nodes * ranks * chips
     node, rank, chip = (lax.axis_index(name) for name in AXES)
-    first_chip, last_chip = chip == 0, chip == chips - 1
-    first, last = first_chip & (rank == 0), last_chip & (rank == ranks - 1)
-    left = (
-        jnp.where(first, jnp.where(node == 0, nodes - 1, node - 1), node),
-        jnp.where(first_chip, jnp.where(rank == 0, ranks - 1, rank - 1), rank),
-        jnp.where(first_chip, chips - 1, chip - 1),
-    )
-    right = (
-        jnp.where(last, jnp.where(node == nodes - 1, 0, node + 1), node),
-        jnp.where(last_chip, jnp.where(rank == ranks - 1, 0, rank + 1), rank),
-        jnp.where(last_chip, 0, chip + 1),
-    )
-    return (node, rank, chip), left, right
-
-
-def on_seam(device, sizes):
-    _, rank, chip = device
-    return ((rank == 0) & (chip == 0)) | ((rank == sizes[1] - 1) & (chip == sizes[2] - 1))
+    place = rank * chips + chip
+    me = node * (ranks * chips) + place
+    left = jnp.where(me == 0, total - 1, me - 1)
+    right = jnp.where(me == total - 1, 0, me + 1)
+    left_seam = (place == 0) | (place == ranks * chips - 1)
+    right_seam = (place == ranks * chips - 1) | (place == ranks * chips - 2)
+    return left, right, left_seam, right_seam
 
 
 def wait_for_rows(count, buffer, semaphore):
@@ -271,14 +261,13 @@
     values, details = rest[: LEVELS + 1], rest[LEVELS + 1 : 2 * LEVELS + 1]
     in_sem, send_sem, recv_sem, level_send_sem, level_recv_sem, here_sem = rest[2 * LEVELS + 1 :]
     rows = x_ref.shape[0]
-    me, left, right = neighbours(sizes)
-    left_seam, right_seam = on_seam(me, sizes), on_seam(right, sizes)
+    left, right, left_seam, right_seam = neighbours(sizes)
     barrier = pltpu.get_barrier_semaphore()
-    pl.semaphore_signal(barrier, inc=1, device_id=left, device_id_type=MESH)
+    pl.semaphore_signal(barrier, inc=1, device_id=left, device_id_type=LOGICAL)
 
     @pl.when(jnp.logical_not(right_seam))
     def _():
-        pl.semaphore_signal(barrier, inc=1, device_id=right, device_id_type=MESH)
+        pl.semaphore_signal(barrier, inc=1, device_id=right, device_id_type=LOGICAL)
 
     def remote(src, dst, sent, come, device):
         return pltpu.make_async_remote_copy(
@@ -287,7 +276,7 @@
             send_sem=sent,
             recv_sem=come,
             device_id=device,
-            device_id_type=MESH,
+            device_id_type=LOGICAL,
         )
 
     low, high = pl.ds(0, COMP), pl.ds(COMP, COMP)
@@ -313,7 +302,7 @@
 
     @pl.when(right_seam)
     def _():
-        pl.semaphore_signal(here_sem, inc=1, device_id=right, device_id_type=MESH)
+        pl.semaphore_signal(here_sem, inc=1, device_id=right, device_id_type=LOGICAL)
 
     @pl.when(jnp.logical_not(left_seam))
     def _():

time: 11.8 us -> 11.8 us (level)
  no operation moved by 1% of the time
where the time goes in v10:
time: 11.8 us; the launch traced here: 11.7 us
  Pallas kernels  11.1 us (94%)
  between operations  0.66 us (6%)
    pallas_call x1, Pallas kernels, per_device(): pl.pallas_call(functools.partial(exchange_kernel, sizes), out_shape=[jax....  10 us
    pallas_call x1, Pallas kernels, per_device(): pl.pallas_call(ends_kernel, out_shape=jax.ShapeDtypeStruct(x.shape, f32),...  1.03 us

profile of v10, /device:TPU:0, one launch (start us, length us, event | category | flops | bytes accessed | tf_op | source)
XLA Modules:
  0.0 11.7 jit_solution(2961474873763955813)
XLA Ops:
  0.7 10.0 %shard_map.28 = (f32[3,256,128]{2,1,0:T(8,128)S(1)}, f32[9,8,128]{2,1,0:T(8,128)S(1)}, s32[8,128]{1,0:T(8,128)S(1)}) custom-call(f32[256,3,128]{2,1,0:T(4,128)} %bitcast.6, s32[1]{0:T(128)S(6)} %copy.3.refine_ref), custom_call_target="tpu_custom_call" | custom-call | tf_op jit(solution)/shard_map/pallas_call | solution.py:399
  10.7 1.0 %shard_map.29 = f32[256,3,128]{2,1,0:T(4,128)} custom-call(f32[3,256,128]{2,1,0:T(8,128)S(1)} %get-tuple-element.8.ob, f32[9,8,128]{2,1,0:T(8,128)S(1)} %get-tuple-element.9.win, s32[8,128]{1,0:T(8,128)S(1)} %get-tuple-element.10.level_ref), custom_call_target="tpu_custom_call" | custom-call | tf_op jit(solution)/shard_map/pallas_call | solution.py:425

commit v11 on v10

--- a/solution.py
+++ b/solution.py
@@ -259,7 +259,7 @@
 
 def exchange_kernel(sizes, x_ref, refine_ref, ob, win, level_ref, xb, near_level, *rest):
     values, details = rest[: LEVELS + 1], rest[LEVELS + 1 : 2 * LEVELS + 1]
-    in_sem, send_sem, recv_sem, level_send_sem, level_recv_sem, here_sem = rest[2 * LEVELS + 1 :]
+    recv_sem, level_recv_sem, here_sem = rest[2 * LEVELS + 1 :]
     rows = x_ref.shape[0]
     left, right, left_seam, right_seam = neighbours(sizes)
     barrier = pltpu.get_barrier_semaphore()
@@ -269,85 +269,89 @@
     def _():
         pl.semaphore_signal(barrier, inc=1, device_id=right, device_id_type=LOGICAL)
 
-    def remote(src, dst, sent, come, device):
-        return pltpu.make_async_remote_copy(
-            src_ref=src,
-            dst_ref=dst,
-            send_sem=sent,
-            recv_sem=come,
-            device_id=device,
-            device_id_type=LOGICAL,
-        )
-
-    low, high = pl.ds(0, COMP), pl.ds(COMP, COMP)
-    level_right = remote(
-        refine_ref, near_level.at[0], level_send_sem, level_recv_sem, right
-    )
-    level_left = remote(refine_ref, near_level.at[1], level_send_sem, level_recv_sem, left)
-    to_right = [
-        remote(
-            x_ref.at[pl.ds(rows - HALO, HALO)], win.at[pl.ds(0, HALO), low, :], send_sem, recv_sem, right
-        ),
-        level_right,
-    ]
-    to_left = [
-        remote(
-            x_ref.at[pl.ds(0, HALO)], win.at[pl.ds(2 * HALO, HALO), high, :], send_sem, recv_sem, left
-        ),
-        level_left,
-    ]
-    pl.semaphore_wait(barrier, jnp.where(left_seam, 1, 2))
-    for copy in to_right:
-        copy.start()
-
-    @pl.when(right_seam)
-    def _():
-        pl.semaphore_signal(here_sem, inc=1, device_id=right, device_id_type=LOGICAL)
-
-    @pl.when(jnp.logical_not(left_seam))
-    def _():
-        for copy in to_left:
-            copy.start()
-
-    for c in range(COMP):
-        pltpu.make_async_copy(x_ref.at[:, c, :], xb.at[c], in_sem).start()
-    pltpu.make_async_copy(xb, xb, in_sem).wait()
-
     lane, sublane = lanes_and_sublanes()
     own = refine_ref[0]
-    for c in range(COMP):
-        win[pl.ds(HALO, 2 * HALO), c, :] = xb[c, pl.ds(0, 2 * HALO), :]
-        win[pl.ds(0, 2 * HALO), COMP + c, :] = xb[c, pl.ds(rows - 2 * HALO, 2 * HALO), :]
-    for c in range(COMP):
-        for half in range(2):
-            values[0][:, 2 * c + half, :] = xb[c, pl.ds(half * LANES, LANES), :].T
-    transform(
-        values, details, lane, jnp.full((8, LANES), own, jnp.int32), before_with_carry, after_with_carry
-    )
-    for c in range(COMP):
-        for half in range(2):
-            ob[c, pl.ds(half * LANES, LANES), :] = values[0][:, 2 * c + half, :].T
-
-    @pl.when(left_seam)
-    def _():
-        pl.semaphore_wait(here_sem, 1)
-        for c in range(COMP):
-            remote(
-                xb.at[c, pl.ds(0, HALO), :],
-                win.at[pl.ds(2 * HALO, HALO), COMP + c, :],
-                send_sem,
-                recv_sem,
-                left,
-            ).start()
-        level_left.start()
-
-    wait_for_rows(2 * HALO * COMP, xb, send_sem)
-    for semaphore in (level_send_sem, level_recv_sem):
-        pltpu.make_async_copy(near_level, near_level, semaphore).wait()
-    wait_for_rows(2 * HALO * COMP, xb, recv_sem)
     side, row = lane % SIDES, lane // SIDES
     from_left = (side < COMP) & (row < HALO)
     from_right = (side >= COMP) & (row >= 2 * HALO)
+
+    def send_and_lift(in_sem, send_sem, level_send_sem):
+        def remote(src, dst, sent, come, device):
+            return pltpu.make_async_remote_copy(
+                src_ref=src,
+                dst_ref=dst,
+                send_sem=sent,
+                recv_sem=come,
+                device_id=device,
+                device_id_type=LOGICAL,
+            )
+
+        low, high = pl.ds(0, COMP), pl.ds(COMP, COMP)
+        level_right = remote(
+            refine_ref, near_level.at[0], level_send_sem, level_recv_sem, right
+        )
+        level_left = remote(refine_ref, near_level.at[1], level_send_sem, level_recv_sem, left)
+        to_right = [
+            remote(
+                x_ref.at[pl.ds(rows - HALO, HALO)], win.at[pl.ds(0, HALO), low, :], send_sem, recv_sem, right
+            ),
+            level_right,
+        ]
+        to_left = [
+            remote(
+                x_ref.at[pl.ds(0, HALO)], win.at[pl.ds(2 * HALO, HALO), high, :], send_sem, recv_sem, left
+            ),
+            level_left,
+        ]
+        pl.semaphore_wait(barrier, jnp.where(left_seam, 1, 2))
+        for copy in to_right:
+            copy.start()
+
+        @pl.when(right_seam)
+        def _():
+            pl.semaphore_signal(here_sem, inc=1, device_id=right, device_id_type=LOGICAL)
+
+        @pl.when(jnp.logical_not(left_seam))
+        def _():
+            for copy in to_left:
+                copy.start()
+
+        for c in range(COMP):
+            pltpu.make_async_copy(x_ref.at[:, c, :], xb.at[c], in_sem).start()
+        pltpu.make_async_copy(xb, xb, in_sem).wait()
+
+        for c in range(COMP):
+            win[pl.ds(HALO, 2 * HALO), c, :] = xb[c, pl.ds(0, 2 * HALO), :]
+            win[pl.ds(0, 2 * HALO), COMP + c, :] = xb[c, pl.ds(rows - 2 * HALO, 2 * HALO), :]
+        for c in range(COMP):
+            for half in range(2):
+                values[0][:, 2 * c + half, :] = xb[c, pl.ds(half * LANES, LANES), :].T
+        transform(
+            values, details, lane, jnp.full((8, LANES), own, jnp.int32), before_with_carry, after_with_carry
+        )
+        for c in range(COMP):
+            for half in range(2):
+                ob[c, pl.ds(half * LANES, LANES), :] = values[0][:, 2 * c + half, :].T
+
+        @pl.when(left_seam)
+        def _():
+            pl.semaphore_wait(here_sem, 1)
+            for c in range(COMP):
+                remote(
+                    xb.at[c, pl.ds(0, HALO), :],
+                    win.at[pl.ds(2 * HALO, HALO), COMP + c, :],
+                    send_sem,
+                    recv_sem,
+                    left,
+                ).start()
+            level_left.start()
+
+        wait_for_rows(2 * HALO * COMP, xb, send_sem)
+        pltpu.make_async_copy(near_level, near_level, level_send_sem).wait()
+
+    pl.run_scoped(send_and_lift, *[pltpu.SemaphoreType.DMA] * 3)
+    pltpu.make_async_copy(near_level, near_level, level_recv_sem).wait()
+    wait_for_rows(2 * HALO * COMP, xb, recv_sem)
     level_ref[...] = jnp.where(
         from_left, near_level[0, 0], jnp.where(from_right, near_level[1, 0], own)
     )
@@ -413,9 +417,6 @@
         + [
             pltpu.SemaphoreType.DMA,
             pltpu.SemaphoreType.DMA,
-            pltpu.SemaphoreType.DMA,
-            pltpu.SemaphoreType.DMA,
-            pltpu.SemaphoreType.DMA,
             pltpu.SemaphoreType.REGULAR,
         ],
         compiler_params=pltpu.CompilerParams(

time: 11.8 us -> 11.8 us (level)
  no operation moved by 1% of the time
where the time goes in v11:
time: 11.8 us; the launch traced here: 11.7 us
  Pallas kernels  11 us (93%)
  between operations  0.66 us (6%)
    pallas_call x1, Pallas kernels, per_device(): pl.pallas_call(functools.partial(exchange_kernel, sizes), out_shape=[jax....  10 us
    pallas_call x1, Pallas kernels, per_device(): pl.pallas_call(ends_kernel, out_shape=jax.ShapeDtypeStruct(x.shape, f32),...  1.03 us

profile of v11, /device:TPU:0, one launch (start us, length us, event | category | flops | bytes accessed | tf_op | source)
XLA Modules:
  0.0 11.7 jit_solution(15180044195342311553)
XLA Ops:
  0.7 10.0 %shard_map.28 = (f32[3,256,128]{2,1,0:T(8,128)S(1)}, f32[9,8,128]{2,1,0:T(8,128)S(1)}, s32[8,128]{1,0:T(8,128)S(1)}) custom-call(f32[256,3,128]{2,1,0:T(4,128)} %bitcast.6, s32[1]{0:T(128)S(6)} %copy.3.refine_ref), custom_call_target="tpu_custom_call" | custom-call | tf_op jit(solution)/shard_map/pallas_call | solution.py:403
  10.7 1.0 %shard_map.29 = f32[256,3,128]{2,1,0:T(4,128)} custom-call(f32[3,256,128]{2,1,0:T(8,128)S(1)} %get-tuple-element.8.ob, f32[9,8,128]{2,1,0:T(8,128)S(1)} %get-tuple-element.9.win, s32[8,128]{1,0:T(8,128)S(1)} %get-tuple-element.10.level_ref), custom_call_target="tpu_custom_call" | custom-call | tf_op jit(solution)/shard_map/pallas_call | solution.py:426

commit v12 on v11

--- a/solution.py
+++ b/solution.py
@@ -128,6 +128,7 @@
 
 PARTS = 8
 PART = LANES // PARTS
+PITCH = PART + 1
 STRIP_ROWS = (72, 24, 16, 16, 16, 16, 40, 16)
 STRIP_FIRST = (-32, -8, -2, -4, -3, -2, -16, -2)
 
@@ -372,13 +373,16 @@
     rows_last = jnp.concatenate([rows_here[WIN - 1 :], rows_here[: WIN - 1]], axis=0)
     cell = lax.broadcasted_iota(jnp.int32, rows_here.shape, 2)
     around = jnp.where(cell < LANES // 2, rows_next, rows_last)
-    turned[:, :used] = rows_here.reshape(used, LANES).T
-    beyond[:, :used] = around.reshape(used, LANES).T
-    inner = [turned[pl.ds(k, PARTS, stride=PART), :] for k in range(PART)]
-    outer = [beyond[pl.ds(k, PARTS, stride=PART), :] for k in range(PART)]
+    for buffer, value in ((turned, rows_here), (beyond, around)):
+        cells = value.reshape(used, LANES).T
+        for part in range(PARTS):
+            buffer[pl.ds(part * PITCH, PART), :used] = cells[part * PART : (part + 1) * PART]
+    inner = [turned[pl.ds(k, PARTS, stride=PITCH), :] for k in range(PART)]
+    outer = [beyond[pl.ds(k, PARTS, stride=PITCH), :] for k in range(PART)]
     for k, value in enumerate(lift_window(inner, outer, level_ref[...], sublane, strips)):
-        turned[pl.ds(k, PARTS, stride=PART), :] = value
-    redone = turned[...].T[HALO * SIDES : 2 * HALO * SIDES]
+        turned[pl.ds(k, PARTS, stride=PITCH), :] = value
+    cells = jnp.concatenate([turned[pl.ds(part * PITCH, PART), :] for part in range(PARTS)], axis=0)
+    redone = cells.T[HALO * SIDES : 2 * HALO * SIDES]
     wout[...] = redone.reshape(HALO, SIDES, LANES)
     for side, first in ((0, 0), (1, rows - HALO)):
         pltpu.make_async_copy(
@@ -430,8 +434,8 @@
         out_specs=pl.BlockSpec(memory_space=pltpu.HBM),
         scratch_shapes=[
             pltpu.VMEM((HALO, SIDES, LANES), f32),
-            pltpu.VMEM((LANES, LANES), f32),
-            pltpu.VMEM((LANES, LANES), f32),
+            pltpu.VMEM((PARTS * PITCH, LANES), f32),
+            pltpu.VMEM((PARTS * PITCH, LANES), f32),
             pltpu.SemaphoreType.DMA,
         ]
         + [

time: 11.8 us -> 11.8 us (level)
  no operation moved by 1% of the time
where the time goes in v12:
time: 11.8 us; the launch traced here: 11.7 us
  Pallas kernels  11 us (93%)
  between operations  0.66 us (6%)
    pallas_call x1, Pallas kernels, per_device(): pl.pallas_call(functools.partial(exchange_kernel, sizes), out_shape=[jax....  10 us
    pallas_call x1, Pallas kernels, per_device(): pl.pallas_call(ends_kernel, out_shape=jax.ShapeDtypeStruct(x.shape, f32),...  1.01 us

profile of v12, /device:TPU:0, one launch (start us, length us, event | category | flops | bytes accessed | tf_op | source)
XLA Modules:
  0.0 11.7 jit_solution(443830002233990286)
XLA Ops:
  0.7 10.0 %shard_map.28 = (f32[3,256,128]{2,1,0:T(8,128)S(1)}, f32[9,8,128]{2,1,0:T(8,128)S(1)}, s32[8,128]{1,0:T(8,128)S(1)}) custom-call(f32[256,3,128]{2,1,0:T(4,128)} %bitcast.6, s32[1]{0:T(128)S(6)} %copy.3.refine_ref), custom_call_target="tpu_custom_call" | custom-call | tf_op jit(solution)/shard_map/pallas_call | solution.py:407
  10.7 1.0 %shard_map.29 = f32[256,3,128]{2,1,0:T(4,128)} custom-call(f32[3,256,128]{2,1,0:T(8,128)S(1)} %get-tuple-element.8.ob, f32[9,8,128]{2,1,0:T(8,128)S(1)} %get-tuple-element.9.win, s32[8,128]{1,0:T(8,128)S(1)} %get-tuple-element.10.level_ref), custom_call_target="tpu_custom_call" | custom-call | tf_op jit(solution)/shard_map/pallas_call | solution.py:430

commit v13 on v12

--- a/solution.py
+++ b/solution.py
@@ -270,12 +270,6 @@
     def _():
         pl.semaphore_signal(barrier, inc=1, device_id=right, device_id_type=LOGICAL)
 
-    lane, sublane = lanes_and_sublanes()
-    own = refine_ref[0]
-    side, row = lane % SIDES, lane // SIDES
-    from_left = (side < COMP) & (row < HALO)
-    from_right = (side >= COMP) & (row >= 2 * HALO)
-
     def send_and_lift(in_sem, send_sem, level_send_sem):
         def remote(src, dst, sent, come, device):
             return pltpu.make_async_remote_copy(
@@ -321,6 +315,8 @@
             pltpu.make_async_copy(x_ref.at[:, c, :], xb.at[c], in_sem).start()
         pltpu.make_async_copy(xb, xb, in_sem).wait()
 
+        lane, sublane = lanes_and_sublanes()
+        own = refine_ref[0]
         for c in range(COMP):
             win[pl.ds(HALO, 2 * HALO), c, :] = xb[c, pl.ds(0, 2 * HALO), :]
             win[pl.ds(0, 2 * HALO), COMP + c, :] = xb[c, pl.ds(rows - 2 * HALO, 2 * HALO), :]
@@ -334,6 +330,11 @@
             for half in range(2):
                 ob[c, pl.ds(half * LANES, LANES), :] = values[0][:, 2 * c + half, :].T
 
+        side = lane & (SIDES - 1)
+        from_left = (side < COMP) & (lane < HALO * SIDES)
+        from_right = (side >= COMP) & (lane >= 2 * HALO * SIDES)
+        level_ref[...] = jnp.where(from_left, 1, jnp.where(from_right, 2, 0))
+
         @pl.when(left_seam)
         def _():
             pl.semaphore_wait(here_sem, 1)
@@ -353,8 +354,9 @@
     pl.run_scoped(send_and_lift, *[pltpu.SemaphoreType.DMA] * 3)
     pltpu.make_async_copy(near_level, near_level, level_recv_sem).wait()
     wait_for_rows(2 * HALO * COMP, xb, recv_sem)
+    whose = level_ref[...]
     level_ref[...] = jnp.where(
-        from_left, near_level[0, 0], jnp.where(from_right, near_level[1, 0], own)
+        whose == 1, near_level[0, 0], jnp.where(whose == 2, near_level[1, 0], refine_ref[0])
     )
 
 

time: 11.8 us -> 11.8 us (level)
  no operation moved by 1% of the time
where the time goes in v13:
time: 11.8 us; the launch traced here: 11.7 us
  Pallas kernels  11 us (93%)
  between operations  0.66 us (6%)
    pallas_call x1, Pallas kernels, per_device(): pl.pallas_call(functools.partial(exchange_kernel, sizes), out_shape=[jax....  10 us
    pallas_call x1, Pallas kernels, per_device(): pl.pallas_call(ends_kernel, out_shape=jax.ShapeDtypeStruct(x.shape, f32),...  1.01 us

profile of v13, /device:TPU:0, one launch (start us, length us, event | category | flops | bytes accessed | tf_op | source)
XLA Modules:
  0.0 11.7 jit_solution(527995985449131923)
XLA Ops:
  0.7 10.0 %shard_map.28 = (f32[3,256,128]{2,1,0:T(8,128)S(1)}, f32[9,8,128]{2,1,0:T(8,128)S(1)}, s32[8,128]{1,0:T(8,128)S(1)}) custom-call(f32[256,3,128]{2,1,0:T(4,128)} %bitcast.6, s32[1]{0:T(128)S(6)} %copy.3.refine_ref), custom_call_target="tpu_custom_call" | custom-call | tf_op jit(solution)/shard_map/pallas_call | solution.py:409
  10.7 1.0 %shard_map.29 = f32[256,3,128]{2,1,0:T(4,128)} custom-call(f32[3,256,128]{2,1,0:T(8,128)S(1)} %get-tuple-element.8.ob, f32[9,8,128]{2,1,0:T(8,128)S(1)} %get-tuple-element.9.win, s32[8,128]{1,0:T(8,128)S(1)} %get-tuple-element.10.level_ref), custom_call_target="tpu_custom_call" | custom-call | tf_op jit(solution)/shard_map/pallas_call | solution.py:432

commit v14 on v13

--- a/solution.py
+++ b/solution.py
@@ -29,7 +29,7 @@
     right = jnp.where(me == total - 1, 0, me + 1)
     left_seam = (place == 0) | (place == ranks * chips - 1)
     right_seam = (place == ranks * chips - 1) | (place == ranks * chips - 2)
-    return left, right, left_seam, right_seam
+    return left, right, left_seam, right_seam, place == ranks * chips - 1
 
 
 def wait_for_rows(count, buffer, semaphore):
@@ -262,9 +262,13 @@
     values, details = rest[: LEVELS + 1], rest[LEVELS + 1 : 2 * LEVELS + 1]
     recv_sem, level_recv_sem, here_sem = rest[2 * LEVELS + 1 :]
     rows = x_ref.shape[0]
-    left, right, left_seam, right_seam = neighbours(sizes)
+    left, right, left_seam, right_seam, last_place = neighbours(sizes)
     barrier = pltpu.get_barrier_semaphore()
-    pl.semaphore_signal(barrier, inc=1, device_id=left, device_id_type=LOGICAL)
+
+    def greet_left():
+        pl.semaphore_signal(barrier, inc=1, device_id=left, device_id_type=LOGICAL)
+
+    pl.when(jnp.logical_not(last_place))(greet_left)
 
     @pl.when(jnp.logical_not(right_seam))
     def _():
@@ -301,6 +305,7 @@
         pl.semaphore_wait(barrier, jnp.where(left_seam, 1, 2))
         for copy in to_right:
             copy.start()
+        pl.when(last_place)(greet_left)
 
         @pl.when(right_seam)
         def _():

time: 11.8 us -> 11.8 us (level)
  no operation moved by 1% of the time
where the time goes in v14:
time: 11.8 us; the launch traced here: 11.7 us
  Pallas kernels  11 us (93%)
  between operations  0.66 us (6%)
    pallas_call x1, Pallas kernels, per_device(): pl.pallas_call(functools.partial(exchange_kernel, sizes), out_shape=[jax....  10 us
    pallas_call x1, Pallas kernels, per_device(): pl.pallas_call(ends_kernel, out_shape=jax.ShapeDtypeStruct(x.shape, f32),...  1.01 us

profile of v14, /device:TPU:0, one launch (start us, length us, event | category | flops | bytes accessed | tf_op | source)
XLA Modules:
  0.0 11.7 jit_solution(17648429946711850876)
XLA Ops:
  0.7 10.0 %shard_map.28 = (f32[3,256,128]{2,1,0:T(8,128)S(1)}, f32[9,8,128]{2,1,0:T(8,128)S(1)}, s32[8,128]{1,0:T(8,128)S(1)}) custom-call(f32[256,3,128]{2,1,0:T(4,128)} %bitcast.6, s32[1]{0:T(128)S(6)} %copy.3.refine_ref), custom_call_target="tpu_custom_call" | custom-call | tf_op jit(solution)/shard_map/pallas_call | solution.py:414
  10.7 1.0 %shard_map.29 = f32[256,3,128]{2,1,0:T(4,128)} custom-call(f32[3,256,128]{2,1,0:T(8,128)S(1)} %get-tuple-element.8.ob, f32[9,8,128]{2,1,0:T(8,128)S(1)} %get-tuple-element.9.win, s32[8,128]{1,0:T(8,128)S(1)} %get-tuple-element.10.level_ref), custom_call_target="tpu_custom_call" | custom-call | tf_op jit(solution)/shard_map/pallas_call | solution.py:437

commit v15 on v13

--- a/solution.py
+++ b/solution.py
@@ -360,7 +360,7 @@
     )
 
 
-def ends_kernel(ob, win, level_ref, out_ref, wout, turned, beyond, out_sem, *strips):
+def write_ends(ob, win, level_ref, out_ref, wout, turned, beyond, strips, out_sem):
     rows = out_ref.shape[0]
     for c in range(COMP):
         pltpu.make_async_copy(
@@ -393,6 +393,13 @@
     pltpu.make_async_copy(ob, ob, out_sem).wait()
 
 
+def ends_kernel(ob, win, level_ref, out_ref, wout, turned, beyond, *strips):
+    pl.run_scoped(
+        functools.partial(write_ends, ob, win, level_ref, out_ref, wout, turned, beyond, strips),
+        pltpu.SemaphoreType.DMA,
+    )
+
+
 def lifting_scratch():
     f32 = jnp.float32
     return [pltpu.VMEM((LANES >> level, 8, LANES), f32) for level in range(LEVELS + 1)] + [
@@ -438,7 +445,6 @@
             pltpu.VMEM((HALO, SIDES, LANES), f32),
             pltpu.VMEM((PARTS * PITCH, LANES), f32),
             pltpu.VMEM((PARTS * PITCH, LANES), f32),
-            pltpu.SemaphoreType.DMA,
         ]
         + [
             pltpu.VMEM((count, LANES), jnp.int32 if first == -16 else f32)

time: 11.8 us -> 11.8 us (level)
  no operation moved by 1% of the time
where the time goes in v15:
time: 11.8 us; the launch traced here: 11.7 us
  Pallas kernels  11 us (93%)
  between operations  0.66 us (6%)
    pallas_call x1, Pallas kernels, per_device(): pl.pallas_call(functools.partial(exchange_kernel, sizes), out_shape=[jax....  10 us
    pallas_call x1, Pallas kernels, per_device(): pl.pallas_call(ends_kernel, out_shape=jax.ShapeDtypeStruct(x.shape, f32),...  1.01 us

profile of v15, /device:TPU:0, one launch (start us, length us, event | category | flops | bytes accessed | tf_op | source)
XLA Modules:
  0.0 11.7 jit_solution(13067528109655504048)
XLA Ops:
  0.7 10.0 %shard_map.28 = (f32[3,256,128]{2,1,0:T(8,128)S(1)}, f32[9,8,128]{2,1,0:T(8,128)S(1)}, s32[8,128]{1,0:T(8,128)S(1)}) custom-call(f32[256,3,128]{2,1,0:T(4,128)} %bitcast.6, s32[1]{0:T(128)S(6)} %copy.3.refine_ref), custom_call_target="tpu_custom_call" | custom-call | tf_op jit(solution)/shard_map/pallas_call | solution.py:416
  10.7 1.0 %shard_map.29 = f32[256,3,128]{2,1,0:T(4,128)} custom-call(f32[3,256,128]{2,1,0:T(8,128)S(1)} %get-tuple-element.8.ob, f32[9,8,128]{2,1,0:T(8,128)S(1)} %get-tuple-element.9.win, s32[8,128]{1,0:T(8,128)S(1)} %get-tuple-element.10.level_ref), custom_call_target="tpu_custom_call" | custom-call | tf_op jit(solution)/shard_map/pallas_call | solution.py:439

commit v16 on v13

--- a/solution.py
+++ b/solution.py
@@ -389,7 +389,7 @@
     for side, first in ((0, 0), (1, rows - HALO)):
         pltpu.make_async_copy(
             wout.at[:, pl.ds(side * COMP, COMP), :], out_ref.at[pl.ds(first, HALO)], out_sem
-        ).start()
+        ).start(priority=1)
     pltpu.make_async_copy(ob, ob, out_sem).wait()
 
 

time: 11.8 us -> 11.8 us (level)
  no operation moved by 1% of the time
where the time goes in v16:
time: 11.8 us; the launch traced here: 11.7 us
  Pallas kernels  11 us (93%)
  between operations  0.66 us (6%)
    pallas_call x1, Pallas kernels, per_device(): pl.pallas_call(functools.partial(exchange_kernel, sizes), out_shape=[jax....  10 us
    pallas_call x1, Pallas kernels, per_device(): pl.pallas_call(ends_kernel, out_shape=jax.ShapeDtypeStruct(x.shape, f32),...  1.01 us

profile of v16, /device:TPU:0, one launch (start us, length us, event | category | flops | bytes accessed | tf_op | source)
XLA Modules:
  0.0 11.7 jit_solution(15049942737025167703)
XLA Ops:
  0.7 10.0 %shard_map.28 = (f32[3,256,128]{2,1,0:T(8,128)S(1)}, f32[9,8,128]{2,1,0:T(8,128)S(1)}, s32[8,128]{1,0:T(8,128)S(1)}) custom-call(f32[256,3,128]{2,1,0:T(4,128)} %bitcast.6, s32[1]{0:T(128)S(6)} %copy.3.refine_ref), custom_call_target="tpu_custom_call" | custom-call | tf_op jit(solution)/shard_map/pallas_call | solution.py:409
  10.7 1.0 %shard_map.29 = f32[256,3,128]{2,1,0:T(4,128)} custom-call(f32[3,256,128]{2,1,0:T(8,128)S(1)} %get-tuple-element.8.ob, f32[9,8,128]{2,1,0:T(8,128)S(1)} %get-tuple-element.9.win, s32[8,128]{1,0:T(8,128)S(1)} %get-tuple-element.10.level_ref), custom_call_target="tpu_custom_call" | custom-call | tf_op jit(solution)/shard_map/pallas_call | solution.py:432
